TPU v7x, 32 devices: a whole 2x2x4 slice. The times are simulated.
32 devices in a mesh: dp: 4 (over y, x), tm: 8 (over z, core).
Axes of the slice: x: 2, y: 2, z: 4, core: 2. Of those that a mesh axis runs over, the one named last changes fastest.
Arguments:
- frames: bfloat16 [16384, 1024], P(('dp', 'tm')), parts along dimension 0, may hold values from -6 to 6
- norm_gain1: float32 [1024], replicated, may hold values from 0.1 to 1.9
- w_qkv1: bfloat16 [1024, 1536], replicated, may hold values from -0.1875 to 0.1875
- log_decay: float32 [8, 16384], P(None, ('dp', 'tm')), parts along dimension 1, may hold values from -0.8 to 0, as said below
- head_gain: float32 [512], replicated, may hold values from 0.1 to 1.9
- w_out1: bfloat16 [512, 1024], replicated, may hold values from -0.25 to 0.25
- norm_gain2: float32 [1024], replicated, may hold values from 0.1 to 1.9
- w_qkv2: bfloat16 [1024, 1536], replicated, may hold values from -4 to 4
- window_ids: int32 [32, 2], P(('dp', 'tm')), parts along dimension 0, may hold values from -1 to 6, as said below
- w_out2: bfloat16 [512, 1024], replicated, may hold values from -0.25 to 0.25
Outputs:
- context: bfloat16 [16384, 1024], P(('dp', 'tm')), parts along dimension 0
There are 4 independent parts, one for each index of `dp`. A program takes and returns all parts, laid end to end along the dimension named above; an argument that names none is the same for every part. Nothing has to cross between parts.
Inputs may be any that keep to these rules, and one draw needn't show every extreme that they name: `log_decay`: values are at most 0; in each head the decay varies over the frames. `window_ids`: row j holds distinct ids of blocks j - 3 to j - 1, or -1 for an empty slot; rows hold different numbers of ids, and some rows none. The last row lists 2 blocks, among them the blocks 1 and 3 before it.
All inputs are finite; a program needn't handle non-finite values.
Results may differ from a plain program's by a relative error of at most 0.0072.
Values may be sent and summed in bfloat16 or wider, within the bound.
A program may use at most 128 MiB of HBM per device.

v0:
```python
import jax
import jax.numpy as jnp
from jax import lax
from jax.sharding import PartitionSpec as P

GROUP = 256
REACH_DEV = 3


def from_behind(block, axis, distance):
    devices = range(lax.axis_size(axis))
    route = [(i - distance, i) for i in devices if i - distance in devices]
    return lax.ppermute(block, axis, route)


def rms_norm(values, gain):
    wide = values.astype(jnp.float32)
    scale = lax.rsqrt(jnp.mean(wide * wide, axis=-1, keepdims=True) + 1e-05)
    return (wide * scale * gain).astype(jnp.bfloat16)


def group_step(state, inputs):
    query, key_part, value, decay = inputs
    cumul = jnp.cumsum(decay, axis=0)
    scores = jnp.einsum("thd,shd->hts", query, key_part, preferred_element_type=jnp.float32)
    trans = cumul.T
    diff = trans[:, :, None] - trans[:, None, :]
    length = decay.shape[0]
    causal = jnp.arange(length)[:, None] >= jnp.arange(length)[None, :]
    weight = jnp.where(causal[None], jnp.exp(jnp.minimum(diff, 0.0)), 0.0)
    mix = (scores * weight).astype(jnp.bfloat16)
    intra = jnp.einsum("hts,shd->thd", mix, value, preferred_element_type=jnp.float32)
    scaled = query.astype(jnp.float32) * jnp.exp(cumul)[:, :, None]
    inter = jnp.einsum("thd,hde->the", scaled, state, precision=lax.Precision.HIGHEST)
    keyed = key_part.astype(jnp.float32) * jnp.exp(cumul[-1][None, :] - cumul)[:, :, None]
    update = jnp.einsum(
        "shd,she->hde", keyed, value.astype(jnp.float32), precision=lax.Precision.HIGHEST
    )
    state = jnp.exp(cumul[-1])[:, None, None] * state + update
    return (state, intra + inter)


def attend_block(query, key_lines, values, mask):
    head_dim = query.shape[-1]
    scores = jnp.einsum(
        "thd,shd->hts", query, key_lines, preferred_element_type=jnp.float32
    ) * head_dim ** (-0.5)
    scores = jnp.where(mask[None], scores, -jnp.inf)
    top = jnp.max(scores, axis=-1, keepdims=True)
    probs = jnp.exp(scores - top)
    total = jnp.sum(probs, axis=-1)
    rounded = probs.astype(jnp.bfloat16)
    summed = jnp.einsum("hts,shd->thd", rounded, values, preferred_element_type=jnp.float32)
    return (summed / total.T[:, :, None]).astype(jnp.bfloat16)


def local(
    frames, norm_gain1, w_qkv1, log_decay, head_gain, w_out1, norm_gain2, w_qkv2, window_ids, w_out2
):
    rows = frames.shape[0]
    width = w_out1.shape[0]
    heads = log_decay.shape[0]
    head_dim = width // heads
    blocks_here = window_ids.shape[0]
    block_len = rows // blocks_here
    h_one = rms_norm(frames, norm_gain1)
    qkv = jnp.dot(h_one, w_qkv1, preferred_element_type=jnp.float32).astype(jnp.bfloat16)
    count = rows // GROUP
    query = qkv[:, :width].reshape(count, GROUP, heads, head_dim)
    key_part = qkv[:, width : 2 * width].reshape(count, GROUP, heads, head_dim)
    value = qkv[:, 2 * width :].reshape(count, GROUP, heads, head_dim)
    decay = log_decay.T.reshape(count, GROUP, heads)
    empty = jnp.zeros((heads, head_dim, head_dim), jnp.float32)
    end_state, lin = lax.scan(group_step, empty, (query, key_part, value, decay))
    running = jnp.cumsum(log_decay, axis=1)
    total_decay = jnp.exp(running[:, -1])

    def chain_step(turn, incoming):
        return from_behind(total_decay[:, None, None] * incoming + end_state, "tm", 1)

    incoming = lax.fori_loop(0, lax.axis_size("tm") - 1, chain_step, empty)
    queries_all = qkv[:, :width].reshape(rows, heads, head_dim).astype(jnp.float32)
    scaled = queries_all * jnp.exp(running.T)[:, :, None]
    carried = jnp.einsum("thd,hde->the", scaled, incoming, precision=lax.Precision.HIGHEST)
    lin = lin.reshape(rows, heads, head_dim) + carried
    normed = lin * lax.rsqrt(jnp.mean(lin * lin, axis=-1, keepdims=True) + 1e-06)
    y_one = (normed.reshape(rows, width) * head_gain).astype(jnp.bfloat16)
    branch = jnp.dot(y_one, w_out1, preferred_element_type=jnp.float32)
    hidden1 = (frames.astype(jnp.float32) + branch).astype(jnp.bfloat16)
    h_two = rms_norm(hidden1, norm_gain2)
    qkv2 = jnp.dot(h_two, w_qkv2, preferred_element_type=jnp.float32).astype(jnp.bfloat16)
    keys_here = qkv2[:, width : 2 * width]
    values_here = qkv2[:, 2 * width :]
    span_needed = REACH_DEV + 1
    key_list = []
    value_list = []
    for offset in range(REACH_DEV, 0, -1):
        got_keys, got_values = from_behind((keys_here, values_here), "tm", offset)
        key_list.append(got_keys)
        value_list.append(got_values)
    pool_keys = jnp.concatenate(key_list + [keys_here], axis=0)
    pool_values = jnp.concatenate(value_list + [values_here], axis=0)
    pool_blocks = span_needed * blocks_here
    pool_keys = pool_keys.reshape(pool_blocks, block_len, heads, head_dim)
    pool_values = pool_values.reshape(pool_blocks, block_len, heads, head_dim)
    first_block = (lax.axis_index("tm") - REACH_DEV) * blocks_here
    causal = jnp.arange(block_len)[:, None] >= jnp.arange(block_len)[None, :]
    ids = window_ids[0]
    valid = ids >= 0
    where_ids = jnp.clip(ids - first_block, 0, pool_blocks - 1)
    own = REACH_DEV * blocks_here
    key_lines = jnp.concatenate(
        [pool_keys[where_ids].reshape(-1, heads, head_dim), pool_keys[own]], axis=0
    )
    values = jnp.concatenate(
        [pool_values[where_ids].reshape(-1, heads, head_dim), pool_values[own]], axis=0
    )
    listed = jnp.broadcast_to(
        jnp.repeat(valid, block_len)[None, :], (block_len, ids.shape[0] * block_len)
    )
    mask = jnp.concatenate([listed, causal], axis=1)
    query_block = qkv2[0:block_len, :width].reshape(block_len, heads, head_dim)
    outputs = attend_block(query_block, key_lines, values, mask).reshape(block_len, width)
    branch2 = jnp.dot(outputs, w_out2, preferred_element_type=jnp.float32)
    return (hidden1.astype(jnp.float32) + branch2).astype(jnp.bfloat16)


def solution(mesh):
    placed = (
        P(("dp", "tm"), None),
        P(),
        P(),
        P(None, ("dp", "tm")),
        P(),
        P(),
        P(),
        P(),
        P(("dp", "tm"), None),
        P(),
    )
    return jax.shard_map(
        local, mesh=mesh, in_specs=placed, out_specs=P(("dp", "tm"), None), check_vma=False
    )
```

profile of v0, /device:TPU:26, one launch (start us, length us, event | category | flops | bytes accessed | tf_op | source)
XLA Modules:
  0.0 236.0 jit_solution(14410335301734719914)
XLA Ops:
  0.0 1.7 fusion.45
  1.7 2.2 reduce-window.16
  4.4 3.1 %convolution_convert_fusion.1 = bf16[512,1536]{1,0:T(8,128)(2,1)S(1)} fusion(bf16[1024,1536]{1,0:T(8,128)(2,1)S(1)} %copy-done, bf16[512,1024]{1,0:T(8,128)(2,1)} %param.14, f32[1024]{0:T(1024)} %param.15, f32[512]{0:T(512)S(1)} %add_rsqrt_fusion.2), kind=kOutput, calls=%fused_computation.62 | convolution fusion | flops 1613496320 | bytes 5773312 | tf_op jit(solution)/shard_map/dot_general | solution.py:67
  7.7 1.3 copy.51
  9.6 0.6 copy.49
  10.8 0.6 copy.48
  11.9 0.6 copy.47
  12.5 31.0 %while.24 = (s32[]{:T(128)}, f32[8,64,64]{2,1,0:T(8,128)S(1)}, f32[2,256,8,64]{1,0,3,2:T(2,128)}, f32[2,256,8]{1,2,0:T(8,128)S(1)}, bf16[2,256,8,64]{1,3,2,0:T(8...) while((s32[]{:T(128)}, f32[8,64,64]{2,1,0:T(8,128)S(1)}, ...), condition=%wide.region_4.5_spmd.clone, body=%wide.region_1.4_spmd.clone.sunk | while | flops 339284000 | bytes 6156619 | solution.py:74
  12.5 0.6 reduce-window.26
  13.8 0.7 convolution_bitcast_fusion.3
  14.5 0.9 fusion.112
  16.5 11.5 %dynamic_update_slice.6 = f32[2,256,8,64]{1,0,3,2:T(2,128)} dynamic-update-slice(f32[2,256,8,64]{1,0,3,2:T(2,128)} %get-tuple-element.236, f32[1,256,8,64]{1,0,3,2:T(1,128)S(1)} %copy.85, s32[]{:T(128)S(6)} %copy.90, s32[]{:T(128)} %constant.24.clone.1..sunk, s32[]{:T(128)} %constant.24.clone.1..sunk, s32[]{:T(128)} %constant.24.clone.1..sunk) | dynamic-update-slice | bytes 1048580 | tf_op jit(solution)/shard_map/while/body/jit(dynamic_update_index_in_dim)/dynamic_update_slice | solution.py:74
  29.3 0.7 convolution_bitcast_fusion.3
  29.9 0.9 fusion.112
  31.9 11.5 %dynamic_update_slice.6 = f32[2,256,8,64]{1,0,3,2:T(2,128)} dynamic-update-slice(f32[2,256,8,64]{1,0,3,2:T(2,128)} %get-tuple-element.236, f32[1,256,8,64]{1,0,3,2:T(1,128)S(1)} %copy.85, s32[]{:T(128)S(6)} %copy.90, s32[]{:T(128)} %constant.24.clone.1..sunk, s32[]{:T(128)} %constant.24.clone.1..sunk, s32[]{:T(128)} %constant.24.clone.1..sunk) | dynamic-update-slice | bytes 1048580 | tf_op jit(solution)/shard_map/while/body/jit(dynamic_update_index_in_dim)/dynamic_update_slice | solution.py:74
  43.5 2.1 reshape.170
  45.6 54.7 %while.23 = (s32[]{:T(128)}, f32[8,64,64]{2,1,0:T(8,128)S(1)}, f32[8]{0:T(128)S(1)}, f32[8,64,64]{2,1,0:T(8,128)S(1)}, s32[]{:T(128)}) while((s32[]{:T(128)}, f32[8,64,64]{2,1,0:T(8,128)S(1)}, f32[8]{0:T(128)S(1)}, f32[8,64,64]{2,1,0:T(8,128)S(1)}, s32[]{:T(128)}) %tuple.53), condition=%wide.region_8.9_spmd, body=%wide.region_7.8_spmd.sunk | while | flops 65538 | bytes 917637 | solution.py:81
  45.7 2.1 collective-permute-start
  47.8 5.8 %collective-permute-done = f32[8,64,64]{2,1,0:T(8,128)S(1)} collective-permute-done((f32[8,64,64]{2,1,0:T(8,128)S(1)}, f32[8,64,64]{2,1,0:T(8,128)S(1)}, u32[]{:S(2)}, u32[]{:S(2)}) %collective-permute-start) | collective-permute-done | bytes 131104 | tf_op jit(solution)/shard_map/while/body/eval_jaxpr/ppermute | solution.py:13
  53.6 1.9 collective-permute-start
  55.5 5.8 %collective-permute-done = f32[8,64,64]{2,1,0:T(8,128)S(1)} collective-permute-done((f32[8,64,64]{2,1,0:T(8,128)S(1)}, f32[8,64,64]{2,1,0:T(8,128)S(1)}, u32[]{:S(2)}, u32[]{:S(2)}) %collective-permute-start) | collective-permute-done | bytes 131104 | tf_op jit(solution)/shard_map/while/body/eval_jaxpr/ppermute | solution.py:13
  61.4 1.9 collective-permute-start
  63.3 5.8 %collective-permute-done = f32[8,64,64]{2,1,0:T(8,128)S(1)} collective-permute-done((f32[8,64,64]{2,1,0:T(8,128)S(1)}, f32[8,64,64]{2,1,0:T(8,128)S(1)}, u32[]{:S(2)}, u32[]{:S(2)}) %collective-permute-start) | collective-permute-done | bytes 131104 | tf_op jit(solution)/shard_map/while/body/eval_jaxpr/ppermute | solution.py:13
  69.2 1.9 collective-permute-start
  71.1 5.8 %collective-permute-done = f32[8,64,64]{2,1,0:T(8,128)S(1)} collective-permute-done((f32[8,64,64]{2,1,0:T(8,128)S(1)}, f32[8,64,64]{2,1,0:T(8,128)S(1)}, u32[]{:S(2)}, u32[]{:S(2)}) %collective-permute-start) | collective-permute-done | bytes 131104 | tf_op jit(solution)/shard_map/while/body/eval_jaxpr/ppermute | solution.py:13
  77.0 1.9 collective-permute-start
  78.9 5.8 %collective-permute-done = f32[8,64,64]{2,1,0:T(8,128)S(1)} collective-permute-done((f32[8,64,64]{2,1,0:T(8,128)S(1)}, f32[8,64,64]{2,1,0:T(8,128)S(1)}, u32[]{:S(2)}, u32[]{:S(2)}) %collective-permute-start) | collective-permute-done | bytes 131104 | tf_op jit(solution)/shard_map/while/body/eval_jaxpr/ppermute | solution.py:13
  84.8 1.9 collective-permute-start
  86.7 5.8 %collective-permute-done = f32[8,64,64]{2,1,0:T(8,128)S(1)} collective-permute-done((f32[8,64,64]{2,1,0:T(8,128)S(1)}, f32[8,64,64]{2,1,0:T(8,128)S(1)}, u32[]{:S(2)}, u32[]{:S(2)}) %collective-permute-start) | collective-permute-done | bytes 131104 | tf_op jit(solution)/shard_map/while/body/eval_jaxpr/ppermute | solution.py:13
  92.5 1.9 collective-permute-start
  94.5 5.8 %collective-permute-done = f32[8,64,64]{2,1,0:T(8,128)S(1)} collective-permute-done((f32[8,64,64]{2,1,0:T(8,128)S(1)}, f32[8,64,64]{2,1,0:T(8,128)S(1)}, u32[]{:S(2)}, u32[]{:S(2)}) %collective-permute-start) | collective-permute-done | bytes 131104 | tf_op jit(solution)/shard_map/while/body/eval_jaxpr/ppermute | solution.py:13
  100.2 1.1 multiply_reduce_fusion
  101.7 0.9 copy-done.4
  102.9 0.9 fusion.49
  103.8 1.0 copy-done.15
  104.9 1.9 convolution_convert_fusion
  106.8 0.9 fusion.86
  107.8 1.9 collective-permute-start.3
  109.7 1.3 collective-permute-start.2
  111.0 1.9 collective-permute-start.6
  112.9 1.3 collective-permute-start.5
  114.2 1.3 collective-permute-start.4
  115.7 1.2 pad_add_fusion
  116.9 2.1 copy.56
  119.0 1.0 copy.61
  120.0 1.1 copy.57
  121.1 22.9 %collective-permute-done.6 = bf16[512,512]{1,0:T(8,128)(2,1)S(1)} collective-permute-done((bf16[512,512]{1,0:T(8,128)(2,1)S(1)}, bf16[512,512]{1,0:T(8,128)(2,1)S(1)}, u32[]{:S(2)}, u32[]{:S(2)}) %collective-permute-start.6) | collective-permute-done | bytes 524320 | tf_op jit(solution)/shard_map/ppermute | solution.py:13
  144.0 1.3 collective-permute-start.1
  145.3 0.8 copy-done.7
  146.1 28.5 %collective-permute-done.4 = bf16[512,512]{1,0:T(8,128)(2,1)} collective-permute-done((bf16[512,512]{1,0:T(8,128)(2,1)S(1)}, bf16[512,512]{1,0:T(8,128)(2,1)}, u32[]{:S(2)}, u32[]{:S(2)}) %collective-permute-start.4) | collective-permute-done | bytes 524320 | tf_op jit(solution)/shard_map/ppermute | solution.py:13
  174.7 1.3 pad_maximum_fusion.1
  176.0 3.7 %reshape.203 = bf16[4,512,8,64]{3,2,1,0:T(8,128)(2,1)} reshape(bf16[2048,512]{1,0:T(8,128)(2,1)S(1)} %pad_maximum_fusion.1) | data formatting | bytes 4194304 | tf_op jit(solution)/shard_map/reshape | solution.py:104
  179.7 4.5 %copy.59 = bf16[4,512,8,64]{1,3,2,0:T(8,128)(2,1)S(1)} copy(bf16[4,512,8,64]{3,2,1,0:T(8,128)(2,1)} %reshape.203) | data formatting | bytes 4194304 | tf_op jit(solution)/shard_map/reshape | solution.py:104
  184.1 0.6 gather_fusion.1
  184.7 1.1 copy.83
  185.9 1.7 pad_maximum_fusion
  187.5 3.7 %reshape.202 = bf16[4,512,8,64]{3,2,1,0:T(8,128)(2,1)} reshape(bf16[2048,512]{1,0:T(8,128)(2,1)S(1)} %pad_maximum_fusion) | data formatting | bytes 4194304 | tf_op jit(solution)/shard_map/reshape | solution.py:105
  191.2 4.5 %copy.54 = bf16[4,512,8,64]{1,3,2,0:T(8,128)(2,1)S(1)} copy(bf16[4,512,8,64]{3,2,1,0:T(8,128)(2,1)} %reshape.202) | data formatting | bytes 4194304 | tf_op jit(solution)/shard_map/reshape | solution.py:105
  195.6 0.6 gather_fusion
  196.4 1.0 copy-done.3
  197.7 12.0 %fusion.39 = (f32[8,512]{1,0:T(8,128)S(1)}, f32[8,512,1536]{2,1,0:T(8,128)}) fusion(pred[512,1536]{1,0:T(8,128)(4,1)S(1)} %copy-done.3, bf16[512,8,64]{0,2,1:T(8,128)(2,1)} %bitcast.119, bf16[512,8,64]{0,2,1:T(8,128)(2,1)} %bitcast.118, bf16[1024,8,64]{0,2,1:T(8,128)(2,1)S(1)} %bitcast.115), kind=kOutput, calls=%fused_computation.49 | convolution fusion | flops 827322368 | bytes 28065792 | tf_op jit(solution)/shard_map/thd,shd->hts/dot_general | solution.py:45
  209.7 11.7 %fusion.40 = f32[8,512]{1,0:T(8,128)S(1)} fusion(f32[8,512,1536]{2,1,0:T(8,128)} %get-tuple-element.151, f32[8,512]{1,0:T(8,128)S(1)} %get-tuple-element.150, pred[512,1536]{1,0:T(8,128)(4,1)S(1)} %copy-done.3), kind=kLoop, calls=%fused_computation.50 | loop fusion | flops 25161728 | bytes 25985024 | tf_op jit(solution)/shard_map/reduce_sum | solution.py:51
  221.4 11.6 %divide_convert_fusion = bf16[512,8,64]{0,2,1:T(8,128)(2,1)S(1)} fusion(f32[8,512,1536]{2,1,0:T(8,128)} %get-tuple-element.151, f32[8,512]{1,0:T(8,128)S(1)} %get-tuple-element.150, pred[512,1536]{1,0:T(8,128)(4,1)S(1)} %copy-done.3, bf16[512,8,64]{0,2,1:T(8,128)(2,1)S(1)} %bitcast.117, bf16[1024,8,64]{0,2,1:T(8,128)(2,1)S(1)} %bitcast.116, ...), kind=kOutput, calls=%fused_computation.85 | convolution fusion | flops 834142208 | bytes 28082176 | tf_op jit(solution)/shard_map/hts,shd->thd/dot_general | solution.py:53
  233.1 2.9 %fusion.52 = bf16[512,1024]{1,0:T(8,128)(2,1)} fusion(bf16[512,1024]{1,0:T(8,128)(2,1)} %copy-done.15, bf16[512,512]{0,1:T(8,128)(2,1)S(1)} %bitcast.123, bf16[512,1024]{1,0:T(8,128)(2,1)S(1)} %copy-done.12), kind=kOutput, calls=%fused_computation.70 | convolution fusion | flops 538443776 | bytes 3670016 | tf_op jit(solution)/shard_map/dot_general | solution.py:124
  (89 shorter events, 8.4 us)
Async XLA Ops:
  0.0 4.4 %copy-start = (bf16[1024,1536]{1,0:T(8,128)(2,1)S(1)}, bf16[1024,1536]{1,0:T(8,128)(2,1)}, u32[]{:S(2)}) copy-start(bf16[1024,1536]{1,0:T(8,128)(2,1)} %param.16) | copy-start | bytes 9437188
  10.7 1.8 copy-start.8
  45.5 54.7 %copy-start.2 = (f32[512,512]{0,1:T(8,128)S(1)}, f32[512,512]{0,1:T(8,128)}, u32[]{:S(2)}) copy-start(f32[512,512]{0,1:T(8,128)} %copy.51) | copy-start | bytes 3145732
  45.7 7.8 %collective-permute-start = (f32[8,64,64]{2,1,0:T(8,128)S(1)}, f32[8,64,64]{2,1,0:T(8,128)S(1)}, u32[]{:S(2)}, u32[]{:S(2)}) collective-permute-start(f32[8,64,64]{2,1,0:T(8,128)S(1)} %multiply_add_fusion.2), channel_id=1, source_target_pairs={{0,1},{1,2},{2,3},{3,4},{4,5},{5,6},{6,7},{8,9},{9,10},{10,11},{11... | collective-permute-start | bytes 393224 | tf_op jit(solution)/shard_map/while/body/eval_jaxpr/ppermute | solution.py:13
  53.6 7.7 %collective-permute-start = (f32[8,64,64]{2,1,0:T(8,128)S(1)}, f32[8,64,64]{2,1,0:T(8,128)S(1)}, u32[]{:S(2)}, u32[]{:S(2)}) collective-permute-start(f32[8,64,64]{2,1,0:T(8,128)S(1)} %multiply_add_fusion.2), channel_id=1, source_target_pairs={{0,1},{1,2},{2,3},{3,4},{4,5},{5,6},{6,7},{8,9},{9,10},{10,11},{11... | collective-permute-start | bytes 393224 | tf_op jit(solution)/shard_map/while/body/eval_jaxpr/ppermute | solution.py:13
  61.4 7.7 %collective-permute-start = (f32[8,64,64]{2,1,0:T(8,128)S(1)}, f32[8,64,64]{2,1,0:T(8,128)S(1)}, u32[]{:S(2)}, u32[]{:S(2)}) collective-permute-start(f32[8,64,64]{2,1,0:T(8,128)S(1)} %multiply_add_fusion.2), channel_id=1, source_target_pairs={{0,1},{1,2},{2,3},{3,4},{4,5},{5,6},{6,7},{8,9},{9,10},{10,11},{11... | collective-permute-start | bytes 393224 | tf_op jit(solution)/shard_map/while/body/eval_jaxpr/ppermute | solution.py:13
  69.2 7.7 %collective-permute-start = (f32[8,64,64]{2,1,0:T(8,128)S(1)}, f32[8,64,64]{2,1,0:T(8,128)S(1)}, u32[]{:S(2)}, u32[]{:S(2)}) collective-permute-start(f32[8,64,64]{2,1,0:T(8,128)S(1)} %multiply_add_fusion.2), channel_id=1, source_target_pairs={{0,1},{1,2},{2,3},{3,4},{4,5},{5,6},{6,7},{8,9},{9,10},{10,11},{11... | collective-permute-start | bytes 393224 | tf_op jit(solution)/shard_map/while/body/eval_jaxpr/ppermute | solution.py:13
  77.0 7.7 %collective-permute-start = (f32[8,64,64]{2,1,0:T(8,128)S(1)}, f32[8,64,64]{2,1,0:T(8,128)S(1)}, u32[]{:S(2)}, u32[]{:S(2)}) collective-permute-start(f32[8,64,64]{2,1,0:T(8,128)S(1)} %multiply_add_fusion.2), channel_id=1, source_target_pairs={{0,1},{1,2},{2,3},{3,4},{4,5},{5,6},{6,7},{8,9},{9,10},{10,11},{11... | collective-permute-start | bytes 393224 | tf_op jit(solution)/shard_map/while/body/eval_jaxpr/ppermute | solution.py:13
  84.8 7.7 %collective-permute-start = (f32[8,64,64]{2,1,0:T(8,128)S(1)}, f32[8,64,64]{2,1,0:T(8,128)S(1)}, u32[]{:S(2)}, u32[]{:S(2)}) collective-permute-start(f32[8,64,64]{2,1,0:T(8,128)S(1)} %multiply_add_fusion.2), channel_id=1, source_target_pairs={{0,1},{1,2},{2,3},{3,4},{4,5},{5,6},{6,7},{8,9},{9,10},{10,11},{11... | collective-permute-start | bytes 393224 | tf_op jit(solution)/shard_map/while/body/eval_jaxpr/ppermute | solution.py:13
  92.5 7.7 %collective-permute-start = (f32[8,64,64]{2,1,0:T(8,128)S(1)}, f32[8,64,64]{2,1,0:T(8,128)S(1)}, u32[]{:S(2)}, u32[]{:S(2)}) collective-permute-start(f32[8,64,64]{2,1,0:T(8,128)S(1)} %multiply_add_fusion.2), channel_id=1, source_target_pairs={{0,1},{1,2},{2,3},{3,4},{4,5},{5,6},{6,7},{8,9},{9,10},{10,11},{11... | collective-permute-start | bytes 393224 | tf_op jit(solution)/shard_map/while/body/eval_jaxpr/ppermute | solution.py:13
  100.2 1.3 copy-start.9
  101.4 1.2 copy-start.4
  101.4 1.5 copy-start.11
  102.9 2.0 copy-start.10
  102.9 2.0 copy-start.13
  103.8 1.0 copy-start.15
  106.8 8.7 %copy-start.14 = (s32[1,2]{1,0:T(1,128)S(1)}, s32[1,2]{1,0:T(1,128)}, u32[]{:S(2)}) copy-start(s32[1,2]{1,0:T(1,128)} %param.22) | copy-start | bytes 28
  107.8 78.1 %collective-permute-start.3 = (bf16[512,512]{1,0:T(8,128)(2,1)}, bf16[512,512]{1,0:T(8,128)(2,1)}, u32[]{:S(2)}, u32[]{:S(2)}) collective-permute-start(bf16[512,512]{1,0:T(8,128)(2,1)} %get-tuple-element.139), channel_id=1, source_target_pairs={{0,1},{1,2},{2,3},{3,4},{4,5},{5,6},{6,7},{8,9},{9,10},{10,11},{11... | collective-permute-start | bytes 1572872 | tf_op jit(solution)/shard_map/ppermute | solution.py:13
  109.7 76.2 %collective-permute-start.2 = (bf16[512,512]{1,0:T(8,128)(2,1)}, bf16[512,512]{1,0:T(8,128)(2,1)}, u32[]{:S(2)}, u32[]{:S(2)}) collective-permute-start(bf16[512,512]{1,0:T(8,128)(2,1)} %get-tuple-element.139), channel_id=1, source_target_pairs={{0,2},{1,3},{2,4},{3,5},{4,6},{5,7},{8,10},{9,11},{10,12},{11,13},... | collective-permute-start | bytes 1572872 | tf_op jit(solution)/shard_map/ppermute | solution.py:13
  111.0 33.0 %collective-permute-start.6 = (bf16[512,512]{1,0:T(8,128)(2,1)S(1)}, bf16[512,512]{1,0:T(8,128)(2,1)S(1)}, u32[]{:S(2)}, u32[]{:S(2)}) collective-permute-start(bf16[512,512]{1,0:T(8,128)(2,1)S(1)} %get-tuple-element.140), channel_id=1, source_target_pairs={{0,1},{1,2},{2,3},{3,4},{4,5},{5,6},{6,7},{8,9},{9,10},{10,11},{11... | collective-permute-start | bytes 1572872 | tf_op jit(solution)/shard_map/ppermute | solution.py:13
  112.9 32.4 %collective-permute-start.5 = (bf16[512,512]{1,0:T(8,128)(2,1)S(1)}, bf16[512,512]{1,0:T(8,128)(2,1)S(1)}, u32[]{:S(2)}, u32[]{:S(2)}) collective-permute-start(bf16[512,512]{1,0:T(8,128)(2,1)S(1)} %get-tuple-element.140), channel_id=1, source_target_pairs={{0,2},{1,3},{2,4},{3,5},{4,6},{5,7},{8,10},{9,11},{10,12},{11,13},... | collective-permute-start | bytes 1572872 | tf_op jit(solution)/shard_map/ppermute | solution.py:13
  114.2 60.4 %collective-permute-start.4 = (bf16[512,512]{1,0:T(8,128)(2,1)S(1)}, bf16[512,512]{1,0:T(8,128)(2,1)}, u32[]{:S(2)}, u32[]{:S(2)}) collective-permute-start(bf16[512,512]{1,0:T(8,128)(2,1)S(1)} %get-tuple-element.140), channel_id=1, source_target_pairs={{0,3},{1,4},{2,5},{3,6},{4,7},{8,11},{9,12},{10,13},{11,14},{12,15... | collective-permute-start | bytes 1572872 | tf_op jit(solution)/shard_map/ppermute | solution.py:13
  144.0 41.9 %collective-permute-start.1 = (bf16[512,512]{1,0:T(8,128)(2,1)}, bf16[512,512]{1,0:T(8,128)(2,1)}, u32[]{:S(2)}, u32[]{:S(2)}) collective-permute-start(bf16[512,512]{1,0:T(8,128)(2,1)} %get-tuple-element.139), channel_id=1, source_target_pairs={{0,3},{1,4},{2,5},{3,6},{4,7},{8,11},{9,12},{10,13},{11,14},{12,15... | collective-permute-start | bytes 1572872 | tf_op jit(solution)/shard_map/ppermute | solution.py:13
  145.3 0.8 copy-start.7
  196.3 1.1 copy-start.3
  196.3 1.5 copy-start.5
  209.7 11.7 %copy-start.6 = (bf16[512,512]{0,1:T(8,128)(2,1)S(1)}, bf16[512,512]{0,1:T(8,128)(2,1)}, u32[]{:S(2)}) copy-start(bf16[512,512]{0,1:T(8,128)(2,1)} %copy.56) | copy-start | bytes 1572868
  221.4 11.7 %copy-start.12 = (bf16[512,1024]{1,0:T(8,128)(2,1)S(1)}, bf16[512,1024]{1,0:T(8,128)(2,1)}, u32[]{:S(2)}) copy-start(bf16[512,1024]{1,0:T(8,128)(2,1)} %param.23) | copy-start | bytes 3145732
  221.4 14.6 %copy-start.1 = (bf16[1024,1536]{1,0:T(8,128)(2,1)S(1)}, bf16[1024,1536]{1,0:T(8,128)(2,1)}, u32[]{:S(2)}) copy-start(bf16[1024,1536]{1,0:T(8,128)(2,1)} %param.16) | copy-start | bytes 9437188
where the time goes:
time: 238 us; the launch traced here: 236 us
  waiting for transfers between devices  91.7 us (39%)
  local copies, waits for them, and re-layouts  60.4 us (25%)
  matrix products  37.8 us (16%)
  other arithmetic  22.8 us (10%)
  starting transfers between devices  22.6 us (9%)
    ppermute x13, waiting for transfers between devices, from_behind(): return lax.ppermute(block, axis, route)  91.7 us
    dynamic_update_slice x4, local copies, waits for them, and re-layouts, local(): lax.scan(group_step, empty, (query, key_part, value, decay))  24.2 us
    ppermute x13, starting transfers between devices, from_behind(): return lax.ppermute(block, axis, route)  22.6 us
    dot_general x1, matrix products, attend_block(): jnp.einsum('thd,shd->hts', query, key_lines, preferred_element_type=jnp.f...  12 us
    reduce_sum x1, other arithmetic, attend_block(): total = jnp.sum(probs, axis=-1)  11.7 us
    dot_general x1, matrix products, attend_block(): jnp.einsum('hts,shd->thd', rounded, values, preferred_element_type=jnp.fl...  11.6 us
    reshape x2, local copies, waits for them, and re-layouts, local(): pool_keys = pool_keys.reshape(pool_blocks, block_len, heads, head_dim)  8.11 us
    reshape x2, local copies, waits for them, and re-layouts, local(): pool_values = pool_values.reshape(pool_blocks, block_len, heads, head_dim)  8.11 us
  transfers between devices with their start and end apart: 13, of which 9 were waited for; matrix products, arithmetic and copies ran while one was open for 7% of the time, Pallas kernels for 0%

commit v1 on v0

v1 whole, which is shorter than its diff:
```python
import functools

import jax
import jax.numpy as jnp
from jax import lax
from jax.experimental import pallas as pl
from jax.experimental.pallas import tpu as pltpu
from jax.sharding import PartitionSpec as P

MESH = pl.DeviceIdType.MESH
TILE = 256
LANES = 128
SCALE2 = 1.4426950408889634


def f32dot(a, b, dims=(((1,), (0,)), ((), ()))):
    return lax.dot_general(a, b, dims, preferred_element_type=jnp.float32)


def tile_at(index, size):
    return pl.ds(pl.multiple_of(index * size, size), size)


def norm_rows(src_ref, gain_ref, dst_ref):
    step = 128

    def body(i, carry):
        rows = tile_at(i, step)
        wide = src_ref[rows, :].astype(jnp.float32)
        scale = lax.rsqrt(jnp.mean(wide * wide, axis=-1, keepdims=True) + 1e-05)
        dst_ref[rows, :] = (wide * scale * gain_ref[...]).astype(jnp.bfloat16)
        return carry

    lax.fori_loop(0, src_ref.shape[0] // step, body, 0)


def layer_one(
    n,
    x_ref, g1_ref, w1_ref, ld_ref, hg_ref, wo_ref, g2_ref, w2_ref,
    hid_ref, qt_ref, kv_ref,
    h_s, qkv_s, y_s, run_s, runt_s, lin_s, x_s, ax_s, e_s, a_s, send_b, recv_b, send_sem, recv_sem,
):
    me = lax.axis_index("tm")
    rows = x_ref.shape[0]
    width = wo_ref.shape[0]
    heads = ld_ref.shape[0]
    pairs = width // LANES
    rounds = max(1, (n - 1).bit_length())
    dists = [1 << r for r in range(rounds)]

    barrier = pltpu.get_barrier_semaphore()
    for dist in dists:
        @pl.when(me + dist < n)
        def _():
            pl.semaphore_signal(barrier, inc=1, device_id={"tm": me + dist}, device_id_type=MESH)

        @pl.when(me >= dist)
        def _():
            pl.semaphore_signal(barrier, inc=1, device_id={"tm": me - dist}, device_id_type=MESH)

    norm_rows(x_ref, g1_ref, h_s)

    def project(j, carry):
        cols = tile_at(j, TILE)
        qkv_s[:, cols] = f32dot(h_s[...], w1_ref[:, cols]).astype(jnp.bfloat16)
        return carry

    lax.fori_loop(width // TILE, 3 * width // TILE, project, 0)

    upper = (
        lax.broadcasted_iota(jnp.int32, (rows, rows), 0)
        <= lax.broadcasted_iota(jnp.int32, (rows, rows), 1)
    ).astype(jnp.float32)
    run = lax.dot_general(
        ld_ref[...], upper, (((1,), (0,)), ((), ())),
        precision=lax.Precision.HIGHEST, preferred_element_type=jnp.float32,
    )
    run_s[...] = run
    runt_s[...] = run.T
    last = run[:, rows - 1 : rows]
    headsel = lax.broadcasted_iota(jnp.int32, (heads, width), 1) // (
        width // heads
    ) == lax.broadcasted_iota(jnp.int32, (heads, width), 0)
    a_row = jnp.sum(jnp.where(headsel, jnp.exp(last), 0.0), axis=0, keepdims=True)
    a_s[...] = a_row
    low = lax.broadcasted_iota(jnp.int32, (1, LANES), 1) < LANES // 2
    left_t = jnp.exp(last - run).T

    for p in range(pairs):
        cols = slice(p * LANES, (p + 1) * LANES)
        kcols = slice(width + p * LANES, width + (p + 1) * LANES)
        vcols = slice(2 * width + p * LANES, 2 * width + (p + 1) * LANES)
        decay = jnp.where(low, left_t[:, 2 * p : 2 * p + 1], left_t[:, 2 * p + 1 : 2 * p + 2])
        keyed = (qkv_s[:, kcols].astype(jnp.float32) * decay).T.astype(jnp.bfloat16)
        full = f32dot(keyed, qkv_s[:, vcols])
        e_s[:, cols] = jnp.where(low, full[: LANES // 2], full[LANES // 2 :])
    x_s[...] = jnp.zeros_like(x_s)
    ax_s[...] = jnp.ones_like(ax_s)

    def send(r, dist):
        w = e_s[...] + a_s[...] * x_s[...]
        aw = a_s[...] * ax_s[...]
        hi = aw.astype(jnp.bfloat16).astype(jnp.float32)
        lo = aw - hi
        row = lax.broadcasted_iota(jnp.int32, (16, width), 0)
        tail = jnp.where(row == 0, hi, jnp.where(row == 1, lo, 0.0))
        send_b[r, 0:64, :] = w.astype(jnp.bfloat16)
        send_b[r, 64:80, :] = tail.astype(jnp.bfloat16)

        @pl.when(me + dist < n)
        def _():
            copy_of(r, dist).start()

    def copy_of(r, dist):
        return pltpu.make_async_remote_copy(
            src_ref=send_b.at[r], dst_ref=recv_b.at[r],
            send_sem=send_sem.at[r], recv_sem=recv_sem.at[r],
            device_id={"tm": me + dist}, device_id_type=MESH,
        )

    def receive(r, dist):
        @pl.when(me >= dist)
        def _():
            copy_of(r, dist).wait_recv()
            got = recv_b[r].astype(jnp.float32)
            x_s[...] = x_s[...] + ax_s[...] * got[0:64]
            ax_s[...] = ax_s[...] * (got[64:65] + got[65:66])

    peers = [me + dist < n for dist in dists] + [me >= dist for dist in dists]
    pl.semaphore_wait(barrier, sum(peer.astype(jnp.int32) for peer in peers))

    def work_query():
        lax.fori_loop(0, width // TILE, project, 0)

    def work_pair(p):
        cols = slice(p * LANES, (p + 1) * LANES)
        kcols = slice(width + p * LANES, width + (p + 1) * LANES)
        vcols = slice(2 * width + p * LANES, 2 * width + (p + 1) * LANES)
        for first in range(0, rows, TILE):
            upto = first + TILE
            parts = []
            query = qkv_s[first:upto, cols]
            keys = qkv_s[0:upto, kcols]
            vals = qkv_s[0:upto, vcols]
            causal = lax.broadcasted_iota(jnp.int32, (TILE, upto), 0) + first >= (
                lax.broadcasted_iota(jnp.int32, (TILE, upto), 1)
            )
            for half in range(2):
                h = 2 * p + half
                keep = low if half == 0 else jnp.logical_not(low)
                mine = jnp.where(keep, query.astype(jnp.float32), 0.0).astype(jnp.bfloat16)
                scores = f32dot(mine, keys, (((1,), (1,)), ((), ())))
                diff = runt_s[first:upto, h : h + 1] - run_s[h : h + 1, 0:upto]
                weight = jnp.where(causal, jnp.exp(jnp.minimum(diff, 0.0)), 0.0)
                parts.append(f32dot((scores * weight).astype(jnp.bfloat16), vals))
            lin_s[first:upto, cols] = jnp.where(low, parts[0], parts[1])

    work = [work_query] + [functools.partial(work_pair, p) for p in range(pairs)]
    send(0, dists[0])
    for r, dist in enumerate(dists):
        take = 1 if r < rounds - 1 else len(work)
        if r == 1:
            take = 2
        for item in work[:take]:
            item()
        work = work[take:]
        receive(r, dist)
        if r + 1 < rounds:
            send(r + 1, dists[r + 1])
    for item in work:
        item()

    for p in range(pairs):
        cols = slice(p * LANES, (p + 1) * LANES)
        packed = x_s[:, cols]
        state = jnp.concatenate(
            [jnp.where(low, packed, 0.0), jnp.where(low, 0.0, packed)], axis=0
        ).astype(jnp.bfloat16)
        grow = jnp.exp(
            jnp.where(low, runt_s[:, 2 * p : 2 * p + 1], runt_s[:, 2 * p + 1 : 2 * p + 2])
        )
        scaled = (qkv_s[:, cols].astype(jnp.float32) * grow).astype(jnp.bfloat16)
        lin = lin_s[:, cols] + f32dot(scaled, state)
        square = lin * lin
        s0 = jnp.sum(jnp.where(low, square, 0.0), axis=-1, keepdims=True)
        s1 = jnp.sum(jnp.where(low, 0.0, square), axis=-1, keepdims=True)
        mean = jnp.where(low, s0, s1) * (1.0 / 64)
        y_s[:, cols] = (lin * lax.rsqrt(mean + 1e-06) * hg_ref[:, cols]).astype(jnp.bfloat16)

    def out_tile(j, carry):
        cols = tile_at(j, TILE)
        branch = f32dot(y_s[...], wo_ref[:, cols])
        hid_ref[:, cols] = (x_ref[:, cols].astype(jnp.float32) + branch).astype(jnp.bfloat16)
        return carry

    lax.fori_loop(0, x_ref.shape[1] // TILE, out_tile, 0)
    norm_rows(hid_ref, g2_ref, h_s)

    tiles = width // TILE

    def q_tile(j, carry):
        block = f32dot(h_s[...], w2_ref[:, tile_at(j, TILE)])
        qt_ref[tile_at(j, TILE), :] = block.T.astype(jnp.bfloat16)
        return carry

    def k_tile(j, carry):
        block = f32dot(h_s[...], w2_ref[:, tile_at(j + tiles, TILE)])
        kv_ref[0, :, tile_at(j, TILE)] = block.astype(jnp.bfloat16)
        return carry

    def v_tile(j, carry):
        block = f32dot(h_s[...], w2_ref[:, tile_at(j + 2 * tiles, TILE)])
        kv_ref[1, tile_at(j, TILE), :] = block.T.astype(jnp.bfloat16)
        return carry

    lax.fori_loop(0, tiles, k_tile, 0)
    lax.fori_loop(0, tiles, v_tile, 0)
    lax.fori_loop(0, tiles, q_tile, 0)
    for r, dist in enumerate(dists):
        @pl.when(me + dist < n)
        def _():
            copy_of(r, dist).wait_send()


def layer_two(
    n,
    qt_ref, kv_ref, hid_ref, bias_ref, wo_ref,
    out_ref,
    buf, m_s, l_s, acc_s, attn_s, own_send, relay_send, recv_sem,
):
    me = lax.axis_index("tm")
    width = wo_ref.shape[0]
    rows = hid_ref.shape[0]
    pairs = width // LANES
    even = lax.rem(me, 2) == 0
    odd = jnp.logical_not(even)

    barrier = pltpu.get_barrier_semaphore()
    links = [
        (jnp.logical_and(even, me >= 2), -2),
        (me >= 1, -1),
        (me + 1 < n, 1),
        (jnp.logical_and(even, me + 2 < n), 2),
    ]
    for cond, shift in links:
        @pl.when(cond)
        def _():
            pl.semaphore_signal(barrier, inc=1, device_id={"tm": me + shift}, device_id_type=MESH)
    pl.semaphore_wait(barrier, sum(cond.astype(jnp.int32) for cond, _ in links))

    def copy_of(src, slot, part, shift, sem):
        return pltpu.make_async_remote_copy(
            src_ref=src, dst_ref=buf.at[slot, part], send_sem=sem,
            recv_sem=recv_sem.at[slot, part],
            device_id={"tm": me + shift}, device_id_type=MESH,
        )

    to_next = me + 1 < n
    to_chip = jnp.logical_and(even, me + 2 < n)

    def own_next(part):
        return copy_of(kv_ref.at[part], 0, part, 1, own_send.at[0, part])

    def own_chip(part):
        return copy_of(kv_ref.at[part], 1, part, 2, own_send.at[1, part])

    relays = [
        (0, 1, 1, jnp.logical_and(even, jnp.logical_and(me >= 1, to_next))),
        (0, 2, 2, jnp.logical_and(to_chip, me >= 1)),
        (1, 2, 1, jnp.logical_and(even, jnp.logical_and(me >= 2, to_next))),
    ]

    def relay(index, part):
        source, slot, shift, _ = relays[index]
        return copy_of(buf.at[source, part], slot, part, shift, relay_send.at[index, part])

    for part in range(2):
        @pl.when(to_next)
        def _():
            own_next(part).start()

        @pl.when(to_chip)
        def _():
            own_chip(part).start()

    low = lax.broadcasted_iota(jnp.int32, (LANES, 1), 0) < LANES // 2
    scale = SCALE2 * 64 ** (-0.5)
    halves = rows // TILE

    def attend(k_ref, v_ref, first, bias):
        def body(i, carry):
            p = i // halves
            hq = lax.rem(i, halves)
            lanes = tile_at(hq, TILE)
            prow = tile_at(p, LANES)
            query = qt_ref[prow, lanes]
            keys = k_ref[:, prow]
            for half in range(2):
                keep = low if half == 0 else jnp.logical_not(low)
                mine = jnp.where(keep, query.astype(jnp.float32), 0.0).astype(jnp.bfloat16)
                s = f32dot(keys, mine) * scale
                if first:
                    seen = lax.broadcasted_iota(jnp.int32, s.shape, 0) <= (
                        lax.broadcasted_iota(jnp.int32, s.shape, 1) + hq * TILE
                    )
                    s = jnp.where(seen, s, -jnp.inf)
                top = jnp.max(s, axis=0, keepdims=True)
                h = 2 * p + half
                vrow = pl.ds(pl.multiple_of(h * 64, 64), 64)
                if first:
                    m_new = top
                    ref_top = top
                else:
                    m_old = m_s[h, :, lanes]
                    shift = bias[:, 0:TILE]
                    m_new = jnp.maximum(m_old, top + shift)
                    ref_top = m_new - shift
                    alpha = jnp.exp2(m_old - m_new)
                w = jnp.exp2(s - ref_top)
                total = jnp.sum(w, axis=0, keepdims=True)
                part = f32dot(v_ref[vrow, :], w.astype(jnp.bfloat16))
                if first:
                    l_s[h, :, lanes] = total
                    acc_s[vrow, lanes] = part
                else:
                    l_s[h, :, lanes] = l_s[h, :, lanes] * alpha + total
                    acc_s[vrow, lanes] = acc_s[vrow, lanes] * alpha + part
                m_s[h, :, lanes] = m_new
            return carry

        lax.fori_loop(0, pairs * halves, body, 0)

    attend(kv_ref.at[0], kv_ref.at[1], True, None)
    for slot in range(3):
        @pl.when(me >= slot + 1)
        def _():
            for part in range(2):
                copy_of(kv_ref.at[part], slot, part, 0, own_send.at[0, part]).wait_recv()
                for index in range(3):
                    if relays[index][0] == slot:
                        @pl.when(relays[index][3])
                        def _():
                            relay(index, part).start()
            attend(buf.at[slot, 0], buf.at[slot, 1], False, bias_ref[slot : slot + 1, :])

    for p in range(pairs):
        prow = slice(p * LANES, (p + 1) * LANES)
        inv = jnp.where(low, 1.0 / l_s[2 * p], 1.0 / l_s[2 * p + 1])
        attn_s[:, prow] = (acc_s[prow, :] * inv).T.astype(jnp.bfloat16)

    def out_tile(j, carry):
        cols = tile_at(j, TILE)
        branch = f32dot(attn_s[...], wo_ref[:, cols])
        out_ref[:, cols] = (hid_ref[:, cols].astype(jnp.float32) + branch).astype(jnp.bfloat16)
        return carry

    lax.fori_loop(0, hid_ref.shape[1] // TILE, out_tile, 0)
    for part in range(2):
        @pl.when(to_next)
        def _():
            own_next(part).wait_send()

        @pl.when(to_chip)
        def _():
            own_chip(part).wait_send()

        for index in range(3):
            @pl.when(relays[index][3])
            def _():
                relay(index, part).wait_send()


def local(
    frames, norm_gain1, w_qkv1, log_decay, head_gain, w_out1, norm_gain2, w_qkv2, window_ids, w_out2
):
    n = lax.axis_size("tm")
    rows, model = frames.shape
    width = w_out1.shape[0]
    heads = log_decay.shape[0]
    rounds = max(1, (n - 1).bit_length())
    vmem = pl.BlockSpec(memory_space=pltpu.VMEM)
    bf, f32 = jnp.bfloat16, jnp.float32
    hidden1, qt, kv = pl.pallas_call(
        functools.partial(layer_one, n),
        out_shape=(
            jax.ShapeDtypeStruct((rows, model), bf),
            jax.ShapeDtypeStruct((width, rows), bf),
            jax.ShapeDtypeStruct((2, width, rows), bf),
        ),
        in_specs=[vmem] * 8,
        out_specs=(vmem, vmem, vmem),
        scratch_shapes=[
            pltpu.VMEM((rows, model), bf),
            pltpu.VMEM((rows, 3 * width), bf),
            pltpu.VMEM((rows, width), bf),
            pltpu.VMEM((heads, rows), f32),
            pltpu.VMEM((rows, heads), f32),
            pltpu.VMEM((rows, width), f32),
            pltpu.VMEM((64, width), f32),
            pltpu.VMEM((1, width), f32),
            pltpu.VMEM((64, width), f32),
            pltpu.VMEM((1, width), f32),
            pltpu.VMEM((rounds, 80, width), bf),
            pltpu.VMEM((rounds, 80, width), bf),
            pltpu.SemaphoreType.DMA((rounds,)),
            pltpu.SemaphoreType.DMA((rounds,)),
        ],
        compiler_params=pltpu.CompilerParams(
            collective_id=0, has_side_effects=True, vmem_limit_bytes=48 * 2**20
        ),
    )(
        frames, norm_gain1.reshape(1, model), w_qkv1, log_decay, head_gain.reshape(1, width),
        w_out1, norm_gain2.reshape(1, model), w_qkv2,
    )
    wanted = lax.axis_index("tm") - jnp.arange(1, 9)
    listed = jnp.any((window_ids[0][None, :] == wanted[:, None]) & (wanted[:, None] >= 0), axis=1)
    bias = jnp.broadcast_to(jnp.where(listed, 0.0, -jnp.inf).astype(f32)[:, None], (8, rows))
    return pl.pallas_call(
        functools.partial(layer_two, n),
        out_shape=jax.ShapeDtypeStruct((rows, model), bf),
        in_specs=[vmem] * 5,
        out_specs=vmem,
        scratch_shapes=[
            pltpu.VMEM((3, 2, width, rows), bf),
            pltpu.VMEM((heads, 1, rows), f32),
            pltpu.VMEM((heads, 1, rows), f32),
            pltpu.VMEM((width, rows), f32),
            pltpu.VMEM((rows, width), bf),
            pltpu.SemaphoreType.DMA((2, 2)),
            pltpu.SemaphoreType.DMA((3, 2)),
            pltpu.SemaphoreType.DMA((3, 2)),
        ],
        compiler_params=pltpu.CompilerParams(
            collective_id=1, has_side_effects=True, vmem_limit_bytes=48 * 2**20
        ),
    )(qt, kv, hidden1, bias, w_out2)


def solution(mesh):
    placed = (
        P(("dp", "tm"), None),
        P(),
        P(),
        P(None, ("dp", "tm")),
        P(),
        P(),
        P(),
        P(),
        P(("dp", "tm"), None),
        P(),
    )
    return jax.shard_map(
        local, mesh=mesh, in_specs=placed, out_specs=P(("dp", "tm"), None), check_vma=False
    )
```

time: 238 us -> 77.3 us (0.32)
  the two profiles are of different devices: /device:TPU:26 before, /device:TPU:22 now
where the time goes in v1:
time: 77.3 us; the launch traced here: 76.9 us
  Pallas kernels  69.8 us (90%)
  local copies, waits for them, and re-layouts  6.27 us (8%)
    pallas_call x1, Pallas kernels, local(): pl.pallas_call(functools.partial(layer_two, n), out_shape=jax.ShapeDtypeS...  47.6 us
    pallas_call x1, Pallas kernels, local(): pl.pallas_call(functools.partial(layer_one, n), out_shape=(jax.ShapeDtype...  22.2 us
    unnamed x15, local copies, waits for them, and re-layouts  6.2 us

profile of v1, /device:TPU:22, one launch (start us, length us, event | category | flops | bytes accessed | tf_op | source)
XLA Modules:
  0.0 76.9 jit_solution(11071200594473380346)
XLA Ops:
  0.0 0.7 and_reduce_fusion
  0.8 0.1 broadcast_in_dim.18.bias_ref
  0.8 0.0 copy-start.1
  0.8 1.2 %copy-done.1 = bf16[512,1024]{1,0:T(8,128)(2,1)S(1)} copy-done((bf16[512,1024]{1,0:T(8,128)(2,1)S(1)}, bf16[512,1024]{1,0:T(8,128)(2,1)}, u32[]{:S(2)}) %copy-start.1) | copy-done | bytes 1048600
  2.1 0.0 copy-start.2
  2.1 1.2 %copy-done.2 = bf16[512,1024]{1,0:T(8,128)(2,1)S(1)} copy-done((bf16[512,1024]{1,0:T(8,128)(2,1)S(1)}, bf16[512,1024]{1,0:T(8,128)(2,1)}, u32[]{:S(2)}) %copy-start.2) | copy-done | bytes 1048600
  3.3 0.0 copy-start.3
  3.3 0.7 copy-done.3
  4.0 0.0 copy-start.4
  4.0 0.7 copy-done.4
  4.7 0.0 copy-start.5
  4.7 0.7 copy-done.5
  5.4 0.0 copy-start.6
  5.4 0.7 copy-done.6
  6.1 0.0 copy-start
  6.1 22.2 %shard_map.100 = (bf16[512,1024]{1,0:T(8,128)(2,1)S(1)}, bf16[512,512]{1,0:T(8,128)(2,1)S(1)}, bf16[2,512,512]{2,1,0:T(8,128)(2,1)S(1)}) custom-call(bf16[512,1024]{1,0:T(8,128)(2,1)S(1)} %copy-done.1, f32[1,1024]{1,0:T(1,128)S(1)} %bitcast.4, bf16[1024,1536]{1,0:T(8,128)(2,1)} %w1_ref.1, f32[8,512]{1,0:T(8,128)S(1)} %copy-done.3, f32[1,512]{1,0:T(1,128)S(1)} %bitcast.6, ...), custom_call_target="tpu_custom_call" | custom-call | tf_op jit(solution)/shard_map/pallas_call | solution.py:383
  28.3 0.0 copy-done
  28.3 47.6 %shard_map.101 = bf16[512,1024]{1,0:T(8,128)(2,1)S(1)} custom-call(bf16[512,512]{1,0:T(8,128)(2,1)S(1)} %get-tuple-element.8.qt_ref, bf16[2,512,512]{2,1,0:T(8,128)(2,1)S(1)} %get-tuple-element.9.kv_ref, bf16[512,1024]{1,0:T(8,128)(2,1)S(1)} %get-tuple-element.10.hid_ref, f32[8,512]{1,0:T(8,128)S(1)} %broadcast_in_dim.18.bias_ref, bf16[512,1024]{1,0:T(8,128)(2,1)S(1)} %copy-done), custom_call_target="tpu_custom_call" | custom-call | tf_op jit(solution)/shard_map/pallas_call | solution.py:418
  75.9 1.0 %copy.12 = bf16[512,1024]{1,0:T(8,128)(2,1)} copy(bf16[512,1024]{1,0:T(8,128)(2,1)S(1)} %shard_map.101) | data formatting | bytes 2097152
  (3 shorter events, 0.0 us)
Async XLA Ops:
  0.8 1.2 %copy-start.1 = (bf16[512,1024]{1,0:T(8,128)(2,1)S(1)}, bf16[512,1024]{1,0:T(8,128)(2,1)}, u32[]{:S(2)}) copy-start(bf16[512,1024]{1,0:T(8,128)(2,1)} %x_ref.1) | copy-start | bytes 3145732
  2.1 1.2 %copy-start.2 = (bf16[512,1024]{1,0:T(8,128)(2,1)S(1)}, bf16[512,1024]{1,0:T(8,128)(2,1)}, u32[]{:S(2)}) copy-start(bf16[512,1024]{1,0:T(8,128)(2,1)} %wo_ref.2) | copy-start | bytes 3145732
  3.3 0.7 copy-start.3
  4.0 0.7 copy-start.4
  4.7 0.7 copy-start.5
  5.4 0.7 copy-start.6
  6.1 22.2 %copy-start = (bf16[512,1024]{1,0:T(8,128)(2,1)S(1)}, bf16[512,1024]{1,0:T(8,128)(2,1)}, u32[]{:S(2)}) copy-start(bf16[512,1024]{1,0:T(8,128)(2,1)} %wo_ref.3) | copy-start | bytes 3145732

commit v2 on v1

--- a/solution.py
+++ b/solution.py
@@ -34,10 +34,12 @@
     lax.fori_loop(0, src_ref.shape[0] // step, body, 0)
 
 
-def layer_one(
+def both_layers(
     n,
-    x_ref, g1_ref, w1_ref, ld_ref, hg_ref, wo_ref, g2_ref, w2_ref,
-    hid_ref, qt_ref, kv_ref,
+    x_hbm, g1_ref, w1_hbm, ld_ref, hg_ref, wo_hbm, g2_ref, w2_hbm, ids_ref, wp_hbm,
+    out_ref,
+    x_ref, w1_ref, wo_ref, w2_ref, wp_ref, hid_ref, qt_ref, k_own, v_own, k_buf, v_buf,
+    m_s, l_s, acc_s, load_sem, own_send, relay_send, kv_recv,
     h_s, qkv_s, y_s, run_s, runt_s, lin_s, x_s, ax_s, e_s, a_s, send_b, recv_b, send_sem, recv_sem,
 ):
     me = lax.axis_index("tm")
@@ -45,7 +47,7 @@
     width = wo_ref.shape[0]
     heads = ld_ref.shape[0]
     pairs = width // LANES
-    rounds = max(1, (n - 1).bit_length())
+    rounds = max(2, (n - 1).bit_length())
     dists = [1 << r for r in range(rounds)]
 
     barrier = pltpu.get_barrier_semaphore()
@@ -58,7 +60,24 @@
         def _():
             pl.semaphore_signal(barrier, inc=1, device_id={"tm": me - dist}, device_id_type=MESH)
 
+    loads = [
+        pltpu.make_async_copy(src, dst, load_sem.at[i])
+        for i, (src, dst) in enumerate(
+            [
+                (x_hbm, x_ref),
+                (w1_hbm.at[:, width:], w1_ref.at[:, width:]),
+                (w1_hbm.at[:, :width], w1_ref.at[:, :width]),
+                (wo_hbm, wo_ref),
+                (w2_hbm, w2_ref),
+                (wp_hbm, wp_ref),
+            ]
+        )
+    ]
+    for load in loads:
+        load.start()
+    loads[0].wait()
     norm_rows(x_ref, g1_ref, h_s)
+    loads[1].wait()
 
     def project(j, carry):
         cols = tile_at(j, TILE)
@@ -130,6 +149,7 @@
     pl.semaphore_wait(barrier, sum(peer.astype(jnp.int32) for peer in peers))
 
     def work_query():
+        loads[2].wait()
         lax.fori_loop(0, width // TILE, project, 0)
 
     def work_pair(p):
@@ -193,110 +213,78 @@
         hid_ref[:, cols] = (x_ref[:, cols].astype(jnp.float32) + branch).astype(jnp.bfloat16)
         return carry
 
+    loads[3].wait()
     lax.fori_loop(0, x_ref.shape[1] // TILE, out_tile, 0)
+    loads[4].wait()
     norm_rows(hid_ref, g2_ref, h_s)
 
-    tiles = width // TILE
-
-    def q_tile(j, carry):
-        block = f32dot(h_s[...], w2_ref[:, tile_at(j, TILE)])
-        qt_ref[tile_at(j, TILE), :] = block.T.astype(jnp.bfloat16)
-        return carry
-
-    def k_tile(j, carry):
-        block = f32dot(h_s[...], w2_ref[:, tile_at(j + tiles, TILE)])
-        kv_ref[0, :, tile_at(j, TILE)] = block.astype(jnp.bfloat16)
-        return carry
-
-    def v_tile(j, carry):
-        block = f32dot(h_s[...], w2_ref[:, tile_at(j + 2 * tiles, TILE)])
-        kv_ref[1, tile_at(j, TILE), :] = block.T.astype(jnp.bfloat16)
-        return carry
-
-    lax.fori_loop(0, tiles, k_tile, 0)
-    lax.fori_loop(0, tiles, v_tile, 0)
-    lax.fori_loop(0, tiles, q_tile, 0)
-    for r, dist in enumerate(dists):
-        @pl.when(me + dist < n)
-        def _():
-            copy_of(r, dist).wait_send()
-
-
-def layer_two(
-    n,
-    qt_ref, kv_ref, hid_ref, bias_ref, wo_ref,
-    out_ref,
-    buf, m_s, l_s, acc_s, attn_s, own_send, relay_send, recv_sem,
-):
-    me = lax.axis_index("tm")
-    width = wo_ref.shape[0]
-    rows = hid_ref.shape[0]
-    pairs = width // LANES
+    groups = width // TILE
     even = lax.rem(me, 2) == 0
-    odd = jnp.logical_not(even)
-
-    barrier = pltpu.get_barrier_semaphore()
-    links = [
-        (jnp.logical_and(even, me >= 2), -2),
-        (me >= 1, -1),
-        (me + 1 < n, 1),
-        (jnp.logical_and(even, me + 2 < n), 2),
-    ]
-    for cond, shift in links:
-        @pl.when(cond)
-        def _():
-            pl.semaphore_signal(barrier, inc=1, device_id={"tm": me + shift}, device_id_type=MESH)
-    pl.semaphore_wait(barrier, sum(cond.astype(jnp.int32) for cond, _ in links))
-
-    def copy_of(src, slot, part, shift, sem):
-        return pltpu.make_async_remote_copy(
-            src_ref=src, dst_ref=buf.at[slot, part], send_sem=sem,
-            recv_sem=recv_sem.at[slot, part],
-            device_id={"tm": me + shift}, device_id_type=MESH,
-        )
-
     to_next = me + 1 < n
     to_chip = jnp.logical_and(even, me + 2 < n)
-
-    def own_next(part):
-        return copy_of(kv_ref.at[part], 0, part, 1, own_send.at[0, part])
-
-    def own_chip(part):
-        return copy_of(kv_ref.at[part], 1, part, 2, own_send.at[1, part])
-
     relays = [
         (0, 1, 1, jnp.logical_and(even, jnp.logical_and(me >= 1, to_next))),
         (0, 2, 2, jnp.logical_and(to_chip, me >= 1)),
         (1, 2, 1, jnp.logical_and(even, jnp.logical_and(me >= 2, to_next))),
     ]
 
-    def relay(index, part):
+    def kv_copies(keys, vals, slot, g, shift, sems):
+        return [
+            pltpu.make_async_remote_copy(
+                src_ref=src, dst_ref=dst.at[slot, g], send_sem=sems.at[i],
+                recv_sem=kv_recv.at[slot, g, i],
+                device_id={"tm": me + shift}, device_id_type=MESH,
+            )
+            for i, (src, dst) in enumerate([(keys, k_buf), (vals, v_buf)])
+        ]
+
+    def own_next(g):
+        return kv_copies(k_own.at[g], v_own.at[g], 0, g, 1, own_send.at[0, g])
+
+    def own_chip(g):
+        return kv_copies(k_own.at[g], v_own.at[g], 1, g, 2, own_send.at[1, g])
+
+    def relay(index, g):
         source, slot, shift, _ = relays[index]
-        return copy_of(buf.at[source, part], slot, part, shift, relay_send.at[index, part])
-
-    for part in range(2):
+        return kv_copies(
+            k_buf.at[source, g], v_buf.at[source, g], slot, g, shift, relay_send.at[index, g]
+        )
+
+    for g in range(groups):
+        lanes = slice(g * TILE, (g + 1) * TILE)
+        kcols = slice(width + g * TILE, width + (g + 1) * TILE)
+        vcols = slice(2 * width + g * TILE, 2 * width + (g + 1) * TILE)
+        k_own[g] = f32dot(h_s[...], w2_ref[:, kcols]).astype(jnp.bfloat16)
+        v_own[g] = f32dot(h_s[...], w2_ref[:, vcols]).T.astype(jnp.bfloat16)
+
+        @pl.when(to_chip)
+        def _():
+            for copy in own_chip(g):
+                copy.start()
+
         @pl.when(to_next)
         def _():
-            own_next(part).start()
-
-        @pl.when(to_chip)
-        def _():
-            own_chip(part).start()
-
-    low = lax.broadcasted_iota(jnp.int32, (LANES, 1), 0) < LANES // 2
+            for copy in own_next(g):
+                copy.start()
+
+    for g in range(groups):
+        lanes = slice(g * TILE, (g + 1) * TILE)
+        qt_ref[lanes, :] = f32dot(h_s[...], w2_ref[:, lanes]).T.astype(jnp.bfloat16)
+
+    tall = lax.broadcasted_iota(jnp.int32, (LANES, 1), 0) < LANES // 2
     scale = SCALE2 * 64 ** (-0.5)
     halves = rows // TILE
-
-    def attend(k_ref, v_ref, first, bias):
+    per_group = TILE // LANES
+
+    def attend(k_ref, v_ref, g, first, bias):
         def body(i, carry):
             p = i // halves
             hq = lax.rem(i, halves)
             lanes = tile_at(hq, TILE)
-            prow = tile_at(p, LANES)
-            query = qt_ref[prow, lanes]
-            keys = k_ref[:, prow]
+            query = qt_ref[tile_at(p + g * per_group, LANES), lanes]
+            keys = k_ref[:, tile_at(p, LANES)]
             for half in range(2):
-                keep = low if half == 0 else jnp.logical_not(low)
+                keep = tall if half == 0 else jnp.logical_not(tall)
                 mine = jnp.where(keep, query.astype(jnp.float32), 0.0).astype(jnp.bfloat16)
                 s = f32dot(keys, mine) * scale
                 if first:
@@ -305,69 +293,90 @@
                     )
                     s = jnp.where(seen, s, -jnp.inf)
                 top = jnp.max(s, axis=0, keepdims=True)
-                h = 2 * p + half
-                vrow = pl.ds(pl.multiple_of(h * 64, 64), 64)
+                h = 2 * (p + g * per_group) + half
+                vrow = pl.ds(pl.multiple_of((2 * p + half) * 64, 64), 64)
+                arow = pl.ds(pl.multiple_of(h * 64, 64), 64)
                 if first:
                     m_new = top
                     ref_top = top
                 else:
                     m_old = m_s[h, :, lanes]
-                    shift = bias[:, 0:TILE]
-                    m_new = jnp.maximum(m_old, top + shift)
-                    ref_top = m_new - shift
+                    m_new = jnp.maximum(m_old, top + bias)
+                    ref_top = m_new - bias
                     alpha = jnp.exp2(m_old - m_new)
                 w = jnp.exp2(s - ref_top)
                 total = jnp.sum(w, axis=0, keepdims=True)
                 part = f32dot(v_ref[vrow, :], w.astype(jnp.bfloat16))
                 if first:
                     l_s[h, :, lanes] = total
-                    acc_s[vrow, lanes] = part
+                    acc_s[arow, lanes] = part
                 else:
                     l_s[h, :, lanes] = l_s[h, :, lanes] * alpha + total
-                    acc_s[vrow, lanes] = acc_s[vrow, lanes] * alpha + part
+                    acc_s[arow, lanes] = acc_s[arow, lanes] * alpha + part
                 m_s[h, :, lanes] = m_new
             return carry
 
-        lax.fori_loop(0, pairs * halves, body, 0)
-
-    attend(kv_ref.at[0], kv_ref.at[1], True, None)
-    for slot in range(3):
+        lax.fori_loop(0, per_group * halves, body, 0)
+
+    for g in range(groups):
+        attend(k_own.at[g], v_own.at[g], g, True, None)
+
+    order = [(slot, g) for g in range(groups) for slot in range(2)]
+    order += [(2, g) for g in range(groups)]
+    for slot, g in order:
         @pl.when(me >= slot + 1)
         def _():
-            for part in range(2):
-                copy_of(kv_ref.at[part], slot, part, 0, own_send.at[0, part]).wait_recv()
-                for index in range(3):
-                    if relays[index][0] == slot:
-                        @pl.when(relays[index][3])
-                        def _():
-                            relay(index, part).start()
-            attend(buf.at[slot, 0], buf.at[slot, 1], False, bias_ref[slot : slot + 1, :])
+            for copy in kv_copies(k_own.at[g], v_own.at[g], slot, g, 0, own_send.at[0, g]):
+                copy.wait_recv()
+            for index in (1, 0, 2):
+                if relays[index][0] == slot:
+                    @pl.when(relays[index][3])
+                    def _():
+                        for copy in relay(index, g):
+                            copy.start()
+            back = me - slot - 1
+            listed = ids_ref[0, 0] == back
+            for j in range(1, ids_ref.shape[1]):
+                listed = jnp.logical_or(listed, ids_ref[0, j] == back)
+            bias = jnp.where(listed, jnp.float32(0.0), jnp.float32(-jnp.inf))
+            attend(k_buf.at[slot, g], v_buf.at[slot, g], g, False, bias)
 
     for p in range(pairs):
         prow = slice(p * LANES, (p + 1) * LANES)
-        inv = jnp.where(low, 1.0 / l_s[2 * p], 1.0 / l_s[2 * p + 1])
-        attn_s[:, prow] = (acc_s[prow, :] * inv).T.astype(jnp.bfloat16)
-
-    def out_tile(j, carry):
+        inv = jnp.where(tall, 1.0 / l_s[2 * p], 1.0 / l_s[2 * p + 1])
+        y_s[:, prow] = (acc_s[prow, :] * inv).T.astype(jnp.bfloat16)
+
+    def last_tile(j, carry):
         cols = tile_at(j, TILE)
-        branch = f32dot(attn_s[...], wo_ref[:, cols])
+        branch = f32dot(y_s[...], wp_ref[:, cols])
         out_ref[:, cols] = (hid_ref[:, cols].astype(jnp.float32) + branch).astype(jnp.bfloat16)
         return carry
 
-    lax.fori_loop(0, hid_ref.shape[1] // TILE, out_tile, 0)
-    for part in range(2):
+    loads[5].wait()
+    lax.fori_loop(0, hid_ref.shape[1] // TILE, last_tile, 0)
+
+    def drain(copies):
+        for copy in copies:
+            copy.wait_send()
+
+    for r, dist in enumerate(dists):
+        @pl.when(me + dist < n)
+        def _():
+            copy_of(r, dist).wait_send()
+
+    for g in range(groups):
         @pl.when(to_next)
         def _():
-            own_next(part).wait_send()
+            drain(own_next(g))
 
         @pl.when(to_chip)
         def _():
-            own_chip(part).wait_send()
+            drain(own_chip(g))
 
         for index in range(3):
             @pl.when(relays[index][3])
             def _():
-                relay(index, part).wait_send()
+                drain(relay(index, g))
 
 
 def local(
@@ -377,19 +386,36 @@
     rows, model = frames.shape
     width = w_out1.shape[0]
     heads = log_decay.shape[0]
-    rounds = max(1, (n - 1).bit_length())
+    rounds = max(2, (n - 1).bit_length())
+    groups = width // TILE
     vmem = pl.BlockSpec(memory_space=pltpu.VMEM)
+    hbm = pl.BlockSpec(memory_space=pl.ANY)
+    smem = pl.BlockSpec(memory_space=pltpu.SMEM)
     bf, f32 = jnp.bfloat16, jnp.float32
-    hidden1, qt, kv = pl.pallas_call(
-        functools.partial(layer_one, n),
-        out_shape=(
-            jax.ShapeDtypeStruct((rows, model), bf),
-            jax.ShapeDtypeStruct((width, rows), bf),
-            jax.ShapeDtypeStruct((2, width, rows), bf),
-        ),
-        in_specs=[vmem] * 8,
-        out_specs=(vmem, vmem, vmem),
+    return pl.pallas_call(
+        functools.partial(both_layers, n),
+        out_shape=jax.ShapeDtypeStruct((rows, model), bf),
+        in_specs=[hbm, vmem, hbm, vmem, vmem, hbm, vmem, hbm, smem, hbm],
+        out_specs=vmem,
         scratch_shapes=[
+            pltpu.VMEM((rows, model), bf),
+            pltpu.VMEM((model, 3 * width), bf),
+            pltpu.VMEM((width, model), bf),
+            pltpu.VMEM((model, 3 * width), bf),
+            pltpu.VMEM((width, model), bf),
+            pltpu.VMEM((rows, model), bf),
+            pltpu.VMEM((width, rows), bf),
+            pltpu.VMEM((groups, rows, TILE), bf),
+            pltpu.VMEM((groups, TILE, rows), bf),
+            pltpu.VMEM((3, groups, rows, TILE), bf),
+            pltpu.VMEM((3, groups, TILE, rows), bf),
+            pltpu.VMEM((heads, 1, rows), f32),
+            pltpu.VMEM((heads, 1, rows), f32),
+            pltpu.VMEM((width, rows), f32),
+            pltpu.SemaphoreType.DMA((6,)),
+            pltpu.SemaphoreType.DMA((2, groups, 2)),
+            pltpu.SemaphoreType.DMA((3, groups, 2)),
+            pltpu.SemaphoreType.DMA((3, groups, 2)),
             pltpu.VMEM((rows, model), bf),
             pltpu.VMEM((rows, 3 * width), bf),
             pltpu.VMEM((rows, width), bf),
@@ -406,34 +432,12 @@
             pltpu.SemaphoreType.DMA((rounds,)),
         ],
         compiler_params=pltpu.CompilerParams(
-            collective_id=0, has_side_effects=True, vmem_limit_bytes=48 * 2**20
+            collective_id=0, has_side_effects=True, vmem_limit_bytes=60 * 2**20
         ),
     )(
         frames, norm_gain1.reshape(1, model), w_qkv1, log_decay, head_gain.reshape(1, width),
-        w_out1, norm_gain2.reshape(1, model), w_qkv2,
+        w_out1, norm_gain2.reshape(1, model), w_qkv2, window_ids, w_out2,
     )
-    wanted = lax.axis_index("tm") - jnp.arange(1, 9)
-    listed = jnp.any((window_ids[0][None, :] == wanted[:, None]) & (wanted[:, None] >= 0), axis=1)
-    bias = jnp.broadcast_to(jnp.where(listed, 0.0, -jnp.inf).astype(f32)[:, None], (8, rows))
-    return pl.pallas_call(
-        functools.partial(layer_two, n),
-        out_shape=jax.ShapeDtypeStruct((rows, model), bf),
-        in_specs=[vmem] * 5,
-        out_specs=vmem,
-        scratch_shapes=[
-            pltpu.VMEM((3, 2, width, rows), bf),
-            pltpu.VMEM((heads, 1, rows), f32),
-            pltpu.VMEM((heads, 1, rows), f32),
-            pltpu.VMEM((width, rows), f32),
-            pltpu.VMEM((rows, width), bf),
-            pltpu.SemaphoreType.DMA((2, 2)),
-            pltpu.SemaphoreType.DMA((3, 2)),
-            pltpu.SemaphoreType.DMA((3, 2)),
-        ],
-        compiler_params=pltpu.CompilerParams(
-            collective_id=1, has_side_effects=True, vmem_limit_bytes=48 * 2**20
-        ),
-    )(qt, kv, hidden1, bias, w_out2)
 
 
 def solution(mesh):

time: 77.3 us -> 61.9 us (0.80)
  the two profiles are of different devices: /device:TPU:22 before, /device:TPU:24 now
where the time goes in v2:
time: 61.9 us; the launch traced here: 61.6 us
  Pallas kernels  59.3 us (96%)
  local copies, waits for them, and re-layouts  2.26 us (4%)
    pallas_call x1, Pallas kernels, local(): pl.pallas_call(functools.partial(both_layers, n), out_shape=jax.ShapeDtyp...  59.3 us
    unnamed x1, local copies, waits for them, and re-layouts  2.26 us

profile of v2, /device:TPU:24, one launch (start us, length us, event | category | flops | bytes accessed | tf_op | source)
XLA Modules:
  0.0 61.6 jit_solution(1785538766651668841)
XLA Ops:
  0.0 59.3 %shard_map.100 = bf16[512,1024]{1,0:T(8,128)(2,1)} custom-call(bf16[512,1024]{1,0:T(8,128)(2,1)} %x_hbm.1, f32[1,1024]{1,0:T(1,128)} %bitcast.3, bf16[1024,1536]{1,0:T(8,128)(2,1)} %w1_hbm.1, f32[8,512]{1,0:T(8,128)} %ld_ref.1, f32[1,512]{1,0:T(1,128)} %bitcast.5, bf16[512,1024]{1,0:T(8,128)(2,1)} %wo_hbm.1, f32[1,1024]{1,0:T(1,128)} %bitcast.4, ...), custom_call_target="tpu_custom_call" | custom-call | tf_op jit(solution)/shard_map/pallas_call | solution.py:395
  59.4 2.3 %copy.12 = bf16[512,1024]{1,0:T(8,128)(2,1)} copy(bf16[512,1024]{1,0:T(8,128)(2,1)} %shard_map.100) | data formatting | bytes 2097152

commit v3 on v2

--- a/solution.py
+++ b/solution.py
@@ -40,6 +40,7 @@
     out_ref,
     x_ref, w1_ref, wo_ref, w2_ref, wp_ref, hid_ref, qt_ref, k_own, v_own, k_buf, v_buf,
     m_s, l_s, acc_s, load_sem, own_send, relay_send, kv_recv,
+    q_far, o_send, o_recv, st_send, st_recv, far_send, far_recv,
     h_s, qkv_s, y_s, run_s, runt_s, lin_s, x_s, ax_s, e_s, a_s, send_b, recv_b, send_sem, recv_sem,
 ):
     me = lax.axis_index("tm")
@@ -224,9 +225,27 @@
     to_chip = jnp.logical_and(even, me + 2 < n)
     relays = [
         (0, 1, 1, jnp.logical_and(even, jnp.logical_and(me >= 1, to_next))),
-        (0, 2, 2, jnp.logical_and(to_chip, me >= 1)),
         (1, 2, 1, jnp.logical_and(even, jnp.logical_and(me >= 2, to_next))),
     ]
+    helps = jnp.logical_and(to_chip, me >= 1)
+    helped = jnp.logical_and(even, me >= 3)
+
+    def query_back(g):
+        return pltpu.make_async_remote_copy(
+            src_ref=qt_ref.at[tile_at(g, TILE)], dst_ref=q_far.at[tile_at(g, TILE)],
+            send_sem=far_send.at[g, 0], recv_sem=far_recv.at[g, 0],
+            device_id={"tm": me - 2}, device_id_type=MESH,
+        )
+
+    def partial_on(g):
+        return [
+            pltpu.make_async_remote_copy(
+                src_ref=src.at[g], dst_ref=dst.at[g],
+                send_sem=far_send.at[g, i], recv_sem=far_recv.at[g, i],
+                device_id={"tm": me + 2}, device_id_type=MESH,
+            )
+            for i, (src, dst) in [(1, (o_send, o_recv)), (2, (st_send, st_recv))]
+        ]
 
     def kv_copies(keys, vals, slot, g, shift, sems):
         return [
@@ -270,6 +289,10 @@
     for g in range(groups):
         lanes = slice(g * TILE, (g + 1) * TILE)
         qt_ref[lanes, :] = f32dot(h_s[...], w2_ref[:, lanes]).T.astype(jnp.bfloat16)
+
+        @pl.when(helped)
+        def _():
+            query_back(g).start()
 
     tall = lax.broadcasted_iota(jnp.int32, (LANES, 1), 0) < LANES // 2
     scale = SCALE2 * 64 ** (-0.5)
@@ -318,27 +341,83 @@
 
         lax.fori_loop(0, per_group * halves, body, 0)
 
+    def attend_far(k_ref, v_ref, g):
+        def body(i, carry):
+            p = i // halves
+            lanes = tile_at(lax.rem(i, halves), TILE)
+            query = q_far[tile_at(p + g * per_group, LANES), lanes]
+            keys = k_ref[:, tile_at(p, LANES)]
+            for half in range(2):
+                keep = tall if half == 0 else jnp.logical_not(tall)
+                mine = jnp.where(keep, query.astype(jnp.float32), 0.0).astype(jnp.bfloat16)
+                s = f32dot(keys, mine) * scale
+                top = jnp.max(s, axis=0, keepdims=True)
+                w = jnp.exp2(s - top)
+                total = jnp.sum(w, axis=0, keepdims=True)
+                h = 2 * p + half
+                vrow = pl.ds(pl.multiple_of(h * 64, 64), 64)
+                part = f32dot(v_ref[vrow, :], w.astype(jnp.bfloat16))
+                o_send[g, vrow, lanes] = (part * (1.0 / total)).astype(jnp.bfloat16)
+                st_send[g, h, :, lanes] = top
+                st_send[g, h + 2 * per_group, :, lanes] = total
+            return carry
+
+        lax.fori_loop(0, per_group * halves, body, 0)
+
+    def merge(g, bias):
+        for j in range(2 * per_group):
+            h = 2 * per_group * g + j
+            arow = slice(h * 64, (h + 1) * 64)
+            m_old = m_s[h]
+            m_far = st_recv[g, j] + bias
+            m_new = jnp.maximum(m_old, m_far)
+            alpha = jnp.exp2(m_old - m_new)
+            beta = st_recv[g, j + 2 * per_group] * jnp.exp2(m_far - m_new)
+            l_s[h] = l_s[h] * alpha + beta
+            far = o_recv[g, j * 64 : (j + 1) * 64, :].astype(jnp.float32)
+            acc_s[arow, :] = acc_s[arow, :] * alpha + far * beta
+
+    def listing(slot):
+        back = me - slot - 1
+        listed = ids_ref[0, 0] == back
+        for j in range(1, ids_ref.shape[1]):
+            listed = jnp.logical_or(listed, ids_ref[0, j] == back)
+        return jnp.where(listed, jnp.float32(0.0), jnp.float32(-jnp.inf))
+
     for g in range(groups):
         attend(k_own.at[g], v_own.at[g], g, True, None)
 
     order = [(slot, g) for g in range(groups) for slot in range(2)]
     order += [(2, g) for g in range(groups)]
     for slot, g in order:
-        @pl.when(me >= slot + 1)
+        here = me >= slot + 1
+        if slot == 2:
+            here = jnp.logical_and(here, jnp.logical_not(even))
+
+            @pl.when(helped)
+            def _():
+                for copy in partial_on(g):
+                    copy.wait_recv()
+                merge(g, listing(2))
+
+        @pl.when(here)
         def _():
             for copy in kv_copies(k_own.at[g], v_own.at[g], slot, g, 0, own_send.at[0, g]):
                 copy.wait_recv()
-            for index in (1, 0, 2):
+            for index in range(len(relays)):
                 if relays[index][0] == slot:
                     @pl.when(relays[index][3])
                     def _():
                         for copy in relay(index, g):
                             copy.start()
-            back = me - slot - 1
-            listed = ids_ref[0, 0] == back
-            for j in range(1, ids_ref.shape[1]):
-                listed = jnp.logical_or(listed, ids_ref[0, j] == back)
-            bias = jnp.where(listed, jnp.float32(0.0), jnp.float32(-jnp.inf))
+            if slot == 0:
+                @pl.when(helps)
+                def _():
+                    query_back(g).wait_recv()
+                    attend_far(k_buf.at[0, g], v_buf.at[0, g], g)
+                    for copy in partial_on(g):
+                        copy.start()
+            bias = listing(slot)
             attend(k_buf.at[slot, g], v_buf.at[slot, g], g, False, bias)
 
     for p in range(pairs):
@@ -373,7 +452,15 @@
         def _():
             drain(own_chip(g))
 
-        for index in range(3):
+        @pl.when(helped)
+        def _():
+            query_back(g).wait_send()
+
+        @pl.when(helps)
+        def _():
+            drain(partial_on(g))
+
+        for index in range(len(relays)):
             @pl.when(relays[index][3])
             def _():
                 drain(relay(index, g))
@@ -389,7 +476,7 @@
     rounds = max(2, (n - 1).bit_length())
     groups = width // TILE
     vmem = pl.BlockSpec(memory_space=pltpu.VMEM)
-    hbm = pl.BlockSpec(memory_space=pl.ANY)
+    hbm = pl.BlockSpec(memory_space=pltpu.HBM)
     smem = pl.BlockSpec(memory_space=pltpu.SMEM)
     bf, f32 = jnp.bfloat16, jnp.float32
     return pl.pallas_call(
@@ -414,8 +501,15 @@
             pltpu.VMEM((width, rows), f32),
             pltpu.SemaphoreType.DMA((6,)),
             pltpu.SemaphoreType.DMA((2, groups, 2)),
+            pltpu.SemaphoreType.DMA((2, groups, 2)),
             pltpu.SemaphoreType.DMA((3, groups, 2)),
-            pltpu.SemaphoreType.DMA((3, groups, 2)),
+            pltpu.VMEM((width, rows), bf),
+            pltpu.VMEM((groups, TILE, rows), bf),
+            pltpu.VMEM((groups, TILE, rows), bf),
+            pltpu.VMEM((groups, heads, 1, rows), f32),
+            pltpu.VMEM((groups, heads, 1, rows), f32),
+            pltpu.SemaphoreType.DMA((groups, 3)),
+            pltpu.SemaphoreType.DMA((groups, 3)),
             pltpu.VMEM((rows, model), bf),
             pltpu.VMEM((rows, 3 * width), bf),
             pltpu.VMEM((rows, width), bf),

time: 61.9 us -> 58.7 us (0.948)
  the two profiles are of different devices: /device:TPU:24 before, /device:TPU:25 now
where the time goes in v3:
time: 58.7 us; the launch traced here: 58.4 us
  Pallas kernels  56.1 us (96%)
  local copies, waits for them, and re-layouts  2.26 us (4%)
    pallas_call x1, Pallas kernels, local(): pl.pallas_call(functools.partial(both_layers, n), out_shape=jax.ShapeDtyp...  56.1 us
    unnamed x1, local copies, waits for them, and re-layouts  2.26 us

profile of v3, /device:TPU:25, one launch (start us, length us, event | category | flops | bytes accessed | tf_op | source)
XLA Modules:
  0.0 58.4 jit_solution(10640656028663883507)
XLA Ops:
  0.0 56.1 %shard_map.100 = bf16[512,1024]{1,0:T(8,128)(2,1)} custom-call(bf16[512,1024]{1,0:T(8,128)(2,1)} %x_hbm.1, f32[1,1024]{1,0:T(1,128)} %bitcast.3, bf16[1024,1536]{1,0:T(8,128)(2,1)} %w1_hbm.1, f32[8,512]{1,0:T(8,128)} %ld_ref.1, f32[1,512]{1,0:T(1,128)} %bitcast.5, bf16[512,1024]{1,0:T(8,128)(2,1)} %wo_hbm.1, f32[1,1024]{1,0:T(1,128)} %bitcast.4, ...), custom_call_target="tpu_custom_call" | custom-call | tf_op jit(solution)/shard_map/pallas_call | solution.py:482
  56.1 2.3 %copy.12 = bf16[512,1024]{1,0:T(8,128)(2,1)} copy(bf16[512,1024]{1,0:T(8,128)(2,1)} %shard_map.100) | data formatting | bytes 2097152

commit v4 on v3

--- a/solution.py
+++ b/solution.py
@@ -36,9 +36,9 @@
 
 def both_layers(
     n,
-    x_hbm, g1_ref, w1_hbm, ld_ref, hg_ref, wo_hbm, g2_ref, w2_hbm, ids_ref, wp_hbm,
-    out_ref,
-    x_ref, w1_ref, wo_ref, w2_ref, wp_ref, hid_ref, qt_ref, k_own, v_own, k_buf, v_buf,
+    x_hbm, g1_ref, w1_hbm, ld_ref, hg_ref, wo_hbm, g2_ref, w2_hbm, ids_ref,
+    hid_ref, attn_ref,
+    x_ref, w1_ref, wo_ref, w2_ref, qt_ref, k_own, v_own, k_buf, v_buf,
     m_s, l_s, acc_s, load_sem, own_send, relay_send, kv_recv,
     q_far, o_send, o_recv, st_send, st_recv, far_send, far_recv,
     h_s, qkv_s, y_s, run_s, runt_s, lin_s, x_s, ax_s, e_s, a_s, send_b, recv_b, send_sem, recv_sem,
@@ -70,7 +70,6 @@
                 (w1_hbm.at[:, :width], w1_ref.at[:, :width]),
                 (wo_hbm, wo_ref),
                 (w2_hbm, w2_ref),
-                (wp_hbm, wp_ref),
             ]
         )
     ]
@@ -288,14 +287,14 @@
 
     for g in range(groups):
         lanes = slice(g * TILE, (g + 1) * TILE)
-        qt_ref[lanes, :] = f32dot(h_s[...], w2_ref[:, lanes]).T.astype(jnp.bfloat16)
+        block = f32dot(h_s[...], w2_ref[:, lanes]) * (SCALE2 * 64 ** (-0.5))
+        qt_ref[lanes, :] = block.T.astype(jnp.bfloat16)
 
         @pl.when(helped)
         def _():
             query_back(g).start()
 
     tall = lax.broadcasted_iota(jnp.int32, (LANES, 1), 0) < LANES // 2
-    scale = SCALE2 * 64 ** (-0.5)
     halves = rows // TILE
     per_group = TILE // LANES
 
@@ -309,7 +308,7 @@
             for half in range(2):
                 keep = tall if half == 0 else jnp.logical_not(tall)
                 mine = jnp.where(keep, query.astype(jnp.float32), 0.0).astype(jnp.bfloat16)
-                s = f32dot(keys, mine) * scale
+                s = f32dot(keys, mine)
                 if first:
                     seen = lax.broadcasted_iota(jnp.int32, s.shape, 0) <= (
                         lax.broadcasted_iota(jnp.int32, s.shape, 1) + hq * TILE
@@ -350,7 +349,7 @@
             for half in range(2):
                 keep = tall if half == 0 else jnp.logical_not(tall)
                 mine = jnp.where(keep, query.astype(jnp.float32), 0.0).astype(jnp.bfloat16)
-                s = f32dot(keys, mine) * scale
+                s = f32dot(keys, mine)
                 top = jnp.max(s, axis=0, keepdims=True)
                 w = jnp.exp2(s - top)
                 total = jnp.sum(w, axis=0, keepdims=True)
@@ -387,52 +386,56 @@
     for g in range(groups):
         attend(k_own.at[g], v_own.at[g], g, True, None)
 
-    order = [(slot, g) for g in range(groups) for slot in range(2)]
-    order += [(2, g) for g in range(groups)]
-    for slot, g in order:
-        here = me >= slot + 1
-        if slot == 2:
-            here = jnp.logical_and(here, jnp.logical_not(even))
-
-            @pl.when(helped)
+    def arrive(slot, g):
+        for copy in kv_copies(k_own.at[g], v_own.at[g], slot, g, 0, own_send.at[0, g]):
+            copy.wait_recv()
+        for index in range(len(relays)):
+            if relays[index][0] == slot:
+                @pl.when(relays[index][3])
+                def _():
+                    for copy in relay(index, g):
+                        copy.start()
+
+    def attend_slot(slot, g):
+        attend(k_buf.at[slot, g], v_buf.at[slot, g], g, False, listing(slot))
+
+    for g in range(groups):
+        @pl.when(me >= 1)
+        def _():
+            arrive(0, g)
+
+            @pl.when(helps)
             def _():
+                query_back(g).wait_recv()
+                attend_far(k_buf.at[0, g], v_buf.at[0, g], g)
                 for copy in partial_on(g):
-                    copy.wait_recv()
-                merge(g, listing(2))
-
-        @pl.when(here)
-        def _():
-            for copy in kv_copies(k_own.at[g], v_own.at[g], slot, g, 0, own_send.at[0, g]):
+                    copy.start()
+
+        @pl.when(me >= 2)
+        def _():
+            arrive(1, g)
+
+        for slot in range(2):
+            @pl.when(me >= slot + 1)
+            def _():
+                attend_slot(slot, g)
+
+    for g in range(groups):
+        @pl.when(helped)
+        def _():
+            for copy in partial_on(g):
                 copy.wait_recv()
-            for index in range(len(relays)):
-                if relays[index][0] == slot:
-                    @pl.when(relays[index][3])
-                    def _():
-                        for copy in relay(index, g):
-                            copy.start()
-            if slot == 0:
-                @pl.when(helps)
-                def _():
-                    query_back(g).wait_recv()
-                    attend_far(k_buf.at[0, g], v_buf.at[0, g], g)
-                    for copy in partial_on(g):
-                        copy.start()
-            bias = listing(slot)
-            attend(k_buf.at[slot, g], v_buf.at[slot, g], g, False, bias)
+            merge(g, listing(2))
+
+        @pl.when(jnp.logical_and(me >= 3, jnp.logical_not(even)))
+        def _():
+            arrive(2, g)
+            attend_slot(2, g)
 
     for p in range(pairs):
         prow = slice(p * LANES, (p + 1) * LANES)
         inv = jnp.where(tall, 1.0 / l_s[2 * p], 1.0 / l_s[2 * p + 1])
-        y_s[:, prow] = (acc_s[prow, :] * inv).T.astype(jnp.bfloat16)
-
-    def last_tile(j, carry):
-        cols = tile_at(j, TILE)
-        branch = f32dot(y_s[...], wp_ref[:, cols])
-        out_ref[:, cols] = (hid_ref[:, cols].astype(jnp.float32) + branch).astype(jnp.bfloat16)
-        return carry
-
-    loads[5].wait()
-    lax.fori_loop(0, hid_ref.shape[1] // TILE, last_tile, 0)
+        attn_ref[:, prow] = (acc_s[prow, :] * inv).T.astype(jnp.bfloat16)
 
     def drain(copies):
         for copy in copies:
@@ -479,18 +482,19 @@
     hbm = pl.BlockSpec(memory_space=pltpu.HBM)
     smem = pl.BlockSpec(memory_space=pltpu.SMEM)
     bf, f32 = jnp.bfloat16, jnp.float32
-    return pl.pallas_call(
+    hidden1, attn = pl.pallas_call(
         functools.partial(both_layers, n),
-        out_shape=jax.ShapeDtypeStruct((rows, model), bf),
-        in_specs=[hbm, vmem, hbm, vmem, vmem, hbm, vmem, hbm, smem, hbm],
-        out_specs=vmem,
+        out_shape=(
+            jax.ShapeDtypeStruct((rows, model), bf),
+            jax.ShapeDtypeStruct((rows, width), bf),
+        ),
+        in_specs=[hbm, vmem, hbm, vmem, vmem, hbm, vmem, hbm, smem],
+        out_specs=(vmem, vmem),
         scratch_shapes=[
             pltpu.VMEM((rows, model), bf),
             pltpu.VMEM((model, 3 * width), bf),
             pltpu.VMEM((width, model), bf),
             pltpu.VMEM((model, 3 * width), bf),
-            pltpu.VMEM((width, model), bf),
-            pltpu.VMEM((rows, model), bf),
             pltpu.VMEM((width, rows), bf),
             pltpu.VMEM((groups, rows, TILE), bf),
             pltpu.VMEM((groups, TILE, rows), bf),
@@ -499,7 +503,7 @@
             pltpu.VMEM((heads, 1, rows), f32),
             pltpu.VMEM((heads, 1, rows), f32),
             pltpu.VMEM((width, rows), f32),
-            pltpu.SemaphoreType.DMA((6,)),
+            pltpu.SemaphoreType.DMA((5,)),
             pltpu.SemaphoreType.DMA((2, groups, 2)),
             pltpu.SemaphoreType.DMA((2, groups, 2)),
             pltpu.SemaphoreType.DMA((3, groups, 2)),
@@ -530,8 +534,10 @@
         ),
     )(
         frames, norm_gain1.reshape(1, model), w_qkv1, log_decay, head_gain.reshape(1, width),
-        w_out1, norm_gain2.reshape(1, model), w_qkv2, window_ids, w_out2,
+        w_out1, norm_gain2.reshape(1, model), w_qkv2, window_ids,
     )
+    branch = jnp.dot(attn, w_out2, preferred_element_type=jnp.float32)
+    return (hidden1.astype(jnp.float32) + branch).astype(jnp.bfloat16)
 
 
 def solution(mesh):

time: 58.7 us -> 61.5 us (1.048)
  matrix products: 0 us -> 3.08 us
  local copies, waits for them, and re-layouts: 2.26 us -> 0.01 us
  Pallas kernels: 56.1 us -> 58.2 us
    dot_general x0 -> x1, matrix products: none -> 3.08 us  [local(): branch = jnp.dot(attn, w_out2, preferred_element_type=jnp.float32)]
    unnamed x1 -> x2, local copies, waits for them, and re-layouts: 2.26 us -> 0.01 us
    pallas_call x1, Pallas kernels: 56.1 us -> 58.2 us  [local(): pl.pallas_call(functools.partial(both_layers, n), out_shape=(jax.ShapeDty...]
where the time goes in v4:
time: 61.5 us; the launch traced here: 61.3 us
  Pallas kernels  58.2 us (95%)
  matrix products  3.08 us (5%)
    pallas_call x1, Pallas kernels, local(): pl.pallas_call(functools.partial(both_layers, n), out_shape=(jax.ShapeDty...  58.2 us
    dot_general x1, matrix products, local(): branch = jnp.dot(attn, w_out2, preferred_element_type=jnp.float32)  3.08 us

profile of v4, /device:TPU:25, one launch (start us, length us, event | category | flops | bytes accessed | tf_op | source)
XLA Modules:
  0.0 61.3 jit_solution(13471586482230205660)
XLA Ops:
  0.0 0.0 copy-start
  0.0 58.2 %shard_map.100 = (bf16[512,1024]{1,0:T(8,128)(2,1)}, bf16[512,512]{1,0:T(8,128)(2,1)}) custom-call(bf16[512,1024]{1,0:T(8,128)(2,1)} %x_hbm.1, f32[1,1024]{1,0:T(1,128)} %bitcast.5, bf16[1024,1536]{1,0:T(8,128)(2,1)} %w1_hbm.1, f32[8,512]{1,0:T(8,128)} %ld_ref.1, f32[1,512]{1,0:T(1,128)} %bitcast.7, bf16[512,1024]{1,0:T(8,128)(2,1)} %wo_hbm.1, ...), custom_call_target="tpu_custom_call" | custom-call | tf_op jit(solution)/shard_map/pallas_call | solution.py:485
  58.2 0.0 copy-done
  58.2 3.1 %add_convert_fusion = bf16[512,1024]{1,0:T(8,128)(2,1)} fusion(bf16[512,1024]{1,0:T(8,128)(2,1)} %get-tuple-element.7, bf16[512,512]{1,0:T(8,128)(2,1)} %get-tuple-element.8, bf16[512,1024]{1,0:T(8,128)(2,1)S(1)} %copy-done), kind=kOutput, calls=%fused_computation | convolution fusion | flops 538443776 | bytes 3670016 | tf_op jit(solution)/shard_map/dot_general | solution.py:539
Async XLA Ops:
  0.0 58.2 %copy-start = (bf16[512,1024]{1,0:T(8,128)(2,1)S(1)}, bf16[512,1024]{1,0:T(8,128)(2,1)}, u32[]{:S(2)}) copy-start(bf16[512,1024]{1,0:T(8,128)(2,1)} %param.19) | copy-start | bytes 3145732

commit v5 on v4

--- a/solution.py
+++ b/solution.py
@@ -36,9 +36,9 @@
 
 def both_layers(
     n,
-    x_hbm, g1_ref, w1_hbm, ld_ref, hg_ref, wo_hbm, g2_ref, w2_hbm, ids_ref,
-    hid_ref, attn_ref,
-    x_ref, w1_ref, wo_ref, w2_ref, qt_ref, k_own, v_own, k_buf, v_buf,
+    x_hbm, g1_ref, w1_hbm, ld_ref, hg_ref, wo_hbm, g2_ref, w2_hbm, ids_ref, wp_hbm,
+    out_ref,
+    x_ref, w1_ref, wo_ref, w2_ref, wp_ref, hid_ref, qt_ref, k_own, v_own, k_buf, v_buf,
     m_s, l_s, acc_s, load_sem, own_send, relay_send, kv_recv,
     q_far, o_send, o_recv, st_send, st_recv, far_send, far_recv,
     h_s, qkv_s, y_s, run_s, runt_s, lin_s, x_s, ax_s, e_s, a_s, send_b, recv_b, send_sem, recv_sem,
@@ -70,6 +70,7 @@
                 (w1_hbm.at[:, :width], w1_ref.at[:, :width]),
                 (wo_hbm, wo_ref),
                 (w2_hbm, w2_ref),
+                (wp_hbm, wp_ref),
             ]
         )
     ]
@@ -386,6 +387,8 @@
     for g in range(groups):
         attend(k_own.at[g], v_own.at[g], g, True, None)
 
+    odd = jnp.logical_not(even)
+
     def arrive(slot, g):
         for copy in kv_copies(k_own.at[g], v_own.at[g], slot, g, 0, own_send.at[0, g]):
             copy.wait_recv()
@@ -399,10 +402,23 @@
     def attend_slot(slot, g):
         attend(k_buf.at[slot, g], v_buf.at[slot, g], g, False, listing(slot))
 
-    for g in range(groups):
-        @pl.when(me >= 1)
-        def _():
+    @pl.when(odd)
+    def _():
+        for g in range(groups):
             arrive(0, g)
+            attend_slot(0, g)
+        for g in range(groups):
+            for slot in (1, 2):
+                @pl.when(me >= slot + 1)
+                def _():
+                    arrive(slot, g)
+                    attend_slot(slot, g)
+
+    @pl.when(jnp.logical_and(even, me >= 2))
+    def _():
+        for g in range(groups):
+            arrive(0, g)
+            arrive(1, g)
 
             @pl.when(helps)
             def _():
@@ -411,14 +427,8 @@
                 for copy in partial_on(g):
                     copy.start()
 
-        @pl.when(me >= 2)
-        def _():
-            arrive(1, g)
-
-        for slot in range(2):
-            @pl.when(me >= slot + 1)
-            def _():
-                attend_slot(slot, g)
+            attend_slot(0, g)
+            attend_slot(1, g)
 
     for g in range(groups):
         @pl.when(helped)
@@ -427,15 +437,19 @@
                 copy.wait_recv()
             merge(g, listing(2))
 
-        @pl.when(jnp.logical_and(me >= 3, jnp.logical_not(even)))
-        def _():
-            arrive(2, g)
-            attend_slot(2, g)
-
     for p in range(pairs):
         prow = slice(p * LANES, (p + 1) * LANES)
         inv = jnp.where(tall, 1.0 / l_s[2 * p], 1.0 / l_s[2 * p + 1])
-        attn_ref[:, prow] = (acc_s[prow, :] * inv).T.astype(jnp.bfloat16)
+        y_s[:, prow] = (acc_s[prow, :] * inv).T.astype(jnp.bfloat16)
+
+    def last_tile(j, carry):
+        cols = tile_at(j, TILE)
+        branch = f32dot(y_s[...], wp_ref[:, cols])
+        out_ref[:, cols] = (hid_ref[:, cols].astype(jnp.float32) + branch).astype(jnp.bfloat16)
+        return carry
+
+    loads[5].wait()
+    lax.fori_loop(0, hid_ref.shape[1] // TILE, last_tile, 0)
 
     def drain(copies):
         for copy in copies:
@@ -482,19 +496,18 @@
     hbm = pl.BlockSpec(memory_space=pltpu.HBM)
     smem = pl.BlockSpec(memory_space=pltpu.SMEM)
     bf, f32 = jnp.bfloat16, jnp.float32
-    hidden1, attn = pl.pallas_call(
+    return pl.pallas_call(
         functools.partial(both_layers, n),
-        out_shape=(
-            jax.ShapeDtypeStruct((rows, model), bf),
-            jax.ShapeDtypeStruct((rows, width), bf),
-        ),
-        in_specs=[hbm, vmem, hbm, vmem, vmem, hbm, vmem, hbm, smem],
-        out_specs=(vmem, vmem),
+        out_shape=jax.ShapeDtypeStruct((rows, model), bf),
+        in_specs=[hbm, vmem, hbm, vmem, vmem, hbm, vmem, hbm, smem, hbm],
+        out_specs=vmem,
         scratch_shapes=[
             pltpu.VMEM((rows, model), bf),
             pltpu.VMEM((model, 3 * width), bf),
             pltpu.VMEM((width, model), bf),
             pltpu.VMEM((model, 3 * width), bf),
+            pltpu.VMEM((width, model), bf),
+            pltpu.VMEM((rows, model), bf),
             pltpu.VMEM((width, rows), bf),
             pltpu.VMEM((groups, rows, TILE), bf),
             pltpu.VMEM((groups, TILE, rows), bf),
@@ -503,7 +516,7 @@
             pltpu.VMEM((heads, 1, rows), f32),
             pltpu.VMEM((heads, 1, rows), f32),
             pltpu.VMEM((width, rows), f32),
-            pltpu.SemaphoreType.DMA((5,)),
+            pltpu.SemaphoreType.DMA((6,)),
             pltpu.SemaphoreType.DMA((2, groups, 2)),
             pltpu.SemaphoreType.DMA((2, groups, 2)),
             pltpu.SemaphoreType.DMA((3, groups, 2)),
@@ -534,10 +547,8 @@
         ),
     )(
         frames, norm_gain1.reshape(1, model), w_qkv1, log_decay, head_gain.reshape(1, width),
-        w_out1, norm_gain2.reshape(1, model), w_qkv2, window_ids,
+        w_out1, norm_gain2.reshape(1, model), w_qkv2, window_ids, w_out2,
     )
-    branch = jnp.dot(attn, w_out2, preferred_element_type=jnp.float32)
-    return (hidden1.astype(jnp.float32) + branch).astype(jnp.bfloat16)
 
 
 def solution(mesh):

time: 61.5 us -> 56.6 us (0.920)
  the two profiles are of different devices: /device:TPU:25 before, /device:TPU:22 now
where the time goes in v5:
time: 56.6 us; the launch traced here: 56.4 us
  Pallas kernels  54.1 us (96%)
  local copies, waits for them, and re-layouts  2.26 us (4%)
    pallas_call x1, Pallas kernels, local(): pl.pallas_call(functools.partial(both_layers, n), out_shape=jax.ShapeDtyp...  54.1 us
    unnamed x1, local copies, waits for them, and re-layouts  2.26 us

profile of v5, /device:TPU:22, one launch (start us, length us, event | category | flops | bytes accessed | tf_op | source)
XLA Modules:
  0.0 56.4 jit_solution(5932669036008462883)
XLA Ops:
  0.0 54.1 %shard_map.100 = bf16[512,1024]{1,0:T(8,128)(2,1)} custom-call(bf16[512,1024]{1,0:T(8,128)(2,1)} %x_hbm.1, f32[1,1024]{1,0:T(1,128)} %bitcast.3, bf16[1024,1536]{1,0:T(8,128)(2,1)} %w1_hbm.1, f32[8,512]{1,0:T(8,128)} %ld_ref.1, f32[1,512]{1,0:T(1,128)} %bitcast.5, bf16[512,1024]{1,0:T(8,128)(2,1)} %wo_hbm.1, f32[1,1024]{1,0:T(1,128)} %bitcast.4, ...), custom_call_target="tpu_custom_call" | custom-call | tf_op jit(solution)/shard_map/pallas_call | solution.py:499
  54.1 2.3 %copy.12 = bf16[512,1024]{1,0:T(8,128)(2,1)} copy(bf16[512,1024]{1,0:T(8,128)(2,1)} %shard_map.100) | data formatting | bytes 2097152

commit v6 on v5

--- a/solution.py
+++ b/solution.py
@@ -418,7 +418,6 @@
     def _():
         for g in range(groups):
             arrive(0, g)
-            arrive(1, g)
 
             @pl.when(helps)
             def _():
@@ -427,6 +426,7 @@
                 for copy in partial_on(g):
                     copy.start()
 
+            arrive(1, g)
             attend_slot(0, g)
             attend_slot(1, g)
 

time: 56.6 us -> 56.3 us (level)
  no operation moved by 1% of the time
where the time goes in v6:
time: 56.3 us; the launch traced here: 56 us
  Pallas kernels  53.8 us (96%)
  local copies, waits for them, and re-layouts  2.26 us (4%)
    pallas_call x1, Pallas kernels, local(): pl.pallas_call(functools.partial(both_layers, n), out_shape=jax.ShapeDtyp...  53.8 us
    unnamed x1, local copies, waits for them, and re-layouts  2.26 us

profile of v6, /device:TPU:22, one launch (start us, length us, event | category | flops | bytes accessed | tf_op | source)
XLA Modules:
  0.0 56.0 jit_solution(15119522713679369689)
XLA Ops:
  0.0 53.8 %shard_map.100 = bf16[512,1024]{1,0:T(8,128)(2,1)} custom-call(bf16[512,1024]{1,0:T(8,128)(2,1)} %x_hbm.1, f32[1,1024]{1,0:T(1,128)} %bitcast.3, bf16[1024,1536]{1,0:T(8,128)(2,1)} %w1_hbm.1, f32[8,512]{1,0:T(8,128)} %ld_ref.1, f32[1,512]{1,0:T(1,128)} %bitcast.5, bf16[512,1024]{1,0:T(8,128)(2,1)} %wo_hbm.1, f32[1,1024]{1,0:T(1,128)} %bitcast.4, ...), custom_call_target="tpu_custom_call" | custom-call | tf_op jit(solution)/shard_map/pallas_call | solution.py:499
  53.8 2.3 %copy.12 = bf16[512,1024]{1,0:T(8,128)(2,1)} copy(bf16[512,1024]{1,0:T(8,128)(2,1)} %shard_map.100) | data formatting | bytes 2097152
